TPU v7x, 32 devices: a whole 2x2x4 slice. The times are simulated.
32 devices in a mesh: dp: 8 (over z, x), tensor: 4 (over y, core).
Axes of the slice: x: 2, y: 2, z: 4, core: 2. Of those that a mesh axis runs over, the one named last changes fastest.
Arguments:
- tokens: bfloat16 [4096, 768], P(('dp', 'tensor')), may hold values from -6 to 6
- attn_gain: bfloat16 [768], P('dp'), may hold values from 0.25 to 1.75
- w_qkv: bfloat16 [3, 768, 768], P(None, 'dp', 'tensor'), may hold values from -14.072913 to 14.072913
- w_out: bfloat16 [768, 768], P('tensor', 'dp'), may hold values from -3 to 3
- mlp_gain: bfloat16 [768], P('dp'), may hold values from 0.25 to 1.75
- w_in: bfloat16 [2, 768, 1152], P(None, 'dp', 'tensor'), may hold values from -0.21875 to 0.21875
- w_down: bfloat16 [1152, 768], P('tensor', 'dp'), may hold values from -0.1875 to 0.1875
- cotangent: bfloat16 [4096, 768], P(('dp', 'tensor')), may hold values from -6 to 6
Outputs:
- out: bfloat16 [4096, 768], P(('dp', 'tensor'))
- input_grad: float32 [4096, 768], P(('dp', 'tensor'))
- attn_gain_grad: float32 [768], P('dp')
- w_qkv_grad: float32 [3, 768, 768], P(None, 'dp', 'tensor')
- w_out_grad: float32 [768, 768], P('tensor', 'dp')
- mlp_gain_grad: float32 [768], P('dp')
- w_in_grad: float32 [2, 768, 1152], P(None, 'dp', 'tensor')
- w_down_grad: float32 [1152, 768], P('tensor', 'dp')
All inputs are finite; a program needn't handle non-finite values.
Results may differ from a plain program's by a relative error of at most 0.013.
Values may be sent and summed in bfloat16 or wider, within the bound.
A program may use at most 64 MiB of HBM per device.

v0:
```python
import jax
import jax.numpy as jnp
from jax import lax
from jax.sharding import PartitionSpec as P

HD = 64
L = 512


NORM_EPS = 1e-05
ROPE_THETA = 160000.0
SQRT_HALF = 0.7071067811865476
GAUSS_NORM = 0.3989422804014327


def rope_tables(row_count):
    position = (jnp.arange(row_count) % L).astype(jnp.float32)
    halves = jnp.arange(HD // 2).astype(jnp.float32)
    inverse = ROPE_THETA ** (-2.0 * halves / HD)
    angles = position[:, None] * inverse[None, :]
    angles = jnp.concatenate([angles, angles], axis=1)
    return (jnp.cos(angles)[:, None, :], jnp.sin(angles)[:, None, :])


def rotate(field_rows, cos_table, sin_table):
    first_half = field_rows[..., : HD // 2]
    second_half = field_rows[..., HD // 2 :]
    turned = jnp.concatenate([-second_half, first_half], axis=-1)
    return field_rows * cos_table + turned * sin_table


def rotate_back(grad_field, cos_table, sin_table):
    scaled = grad_field * sin_table
    turned = jnp.concatenate([scaled[..., HD // 2 :], -scaled[..., : HD // 2]], axis=-1)
    return grad_field * cos_table + turned


def normalize(values):
    centred = values - jnp.mean(values, axis=-1, keepdims=True)
    inv_std = lax.rsqrt(jnp.mean(centred * centred, axis=-1, keepdims=True) + NORM_EPS)
    return (centred * inv_std, inv_std)


def normalize_back(grad_norm, normed, inv_std, gain_row):
    gain_part = jnp.sum(grad_norm * normed, axis=0)
    scaled = grad_norm * gain_row
    centred = scaled - jnp.mean(scaled, axis=-1, keepdims=True)
    grad_in = inv_std * (centred - normed * jnp.mean(scaled * normed, axis=-1, keepdims=True))
    return (grad_in, gain_part)


def gelu_pair(inputs):
    normal_cdf = 0.5 * (1.0 + lax.erf(inputs * SQRT_HALF))
    return (inputs * normal_cdf, normal_cdf + inputs * jnp.exp(-0.5 * inputs * inputs) * GAUSS_NORM)


def attend(queries, key_rows, value_rows):
    score_scale = HD ** (-0.5)
    scores = (
        jnp.einsum("qhd,khd->hqk", queries, key_rows, preferred_element_type=jnp.float32)
        * score_scale
    )
    row_max = jnp.max(scores, axis=-1, keepdims=True)
    log_total = row_max + jnp.log(jnp.sum(jnp.exp(scores - row_max), axis=-1, keepdims=True))
    weights = jnp.exp(scores - log_total).astype(jnp.bfloat16)
    attn_mix = jnp.einsum(
        "hqk,khd->qhd", weights, value_rows, preferred_element_type=jnp.float32
    ).astype(jnp.bfloat16)
    return (attn_mix, log_total)


def attend_back(queries, key_rows, value_rows, attn_mix, grad_mix, log_total):
    score_scale = HD ** (-0.5)
    scores = (
        jnp.einsum("qhd,khd->hqk", queries, key_rows, preferred_element_type=jnp.float32)
        * score_scale
    )
    probabilities = jnp.exp(scores - log_total)
    grad_probs = jnp.einsum(
        "qhd,khd->hqk", grad_mix, value_rows, preferred_element_type=jnp.float32
    )
    row_delta = jnp.sum(grad_mix.astype(jnp.float32) * attn_mix.astype(jnp.float32), axis=-1)
    grad_scores = (probabilities * (grad_probs - jnp.transpose(row_delta)[:, :, None])).astype(
        jnp.bfloat16
    )
    prob_rounded = probabilities.astype(jnp.bfloat16)
    grad_values = jnp.einsum(
        "hqk,qhd->khd", prob_rounded, grad_mix, preferred_element_type=jnp.float32
    )
    grad_queries = (
        jnp.einsum("hqk,khd->qhd", grad_scores, key_rows, preferred_element_type=jnp.float32)
        * score_scale
    )
    grad_keys = (
        jnp.einsum("hqk,qhd->khd", grad_scores, queries, preferred_element_type=jnp.float32)
        * score_scale
    )
    return (grad_queries, grad_keys, grad_values)


def body(tokens, attn_gain, w_qkv, w_out, mlp_gain, w_in, w_down, cotangent):
    attn_full, qkv_weight, out_weight = (
        lax.all_gather(attn_gain, "dp", axis=0, tiled=True),
        lax.all_gather(w_qkv, "dp", axis=1, tiled=True),
        lax.all_gather(w_out, "dp", axis=1, tiled=True),
    )
    mlp_full, in_weight, down_weight = (
        lax.all_gather(mlp_gain, "dp", axis=0, tiled=True),
        lax.all_gather(w_in, "dp", axis=1, tiled=True),
        lax.all_gather(w_down, "dp", axis=1, tiled=True),
    )
    residual = tokens.astype(jnp.float32)
    normed_one, inv_one = normalize(residual)
    ln_one = (normed_one * attn_full.astype(jnp.float32)).astype(jnp.bfloat16)
    rows_one = lax.all_gather(ln_one, "tensor", axis=0, tiled=True)
    row_count = rows_one.shape[0]
    head_count = qkv_weight.shape[2] // HD
    head_shape = (row_count, head_count, HD)
    seq_shape = (row_count // L, L, head_count, HD)
    flat_shape = (row_count, head_count * HD)
    cos_table, sin_table = rope_tables(row_count)
    projected = jnp.einsum("td,ide->ite", rows_one, qkv_weight, preferred_element_type=jnp.float32)
    queries = (
        rotate(projected[0].reshape(head_shape), cos_table, sin_table)
        .astype(jnp.bfloat16)
        .reshape(seq_shape)
    )
    key_rows = (
        rotate(projected[1].reshape(head_shape), cos_table, sin_table)
        .astype(jnp.bfloat16)
        .reshape(seq_shape)
    )
    value_rows = projected[2].astype(jnp.bfloat16).reshape(seq_shape)
    attn_mix, log_total = lax.map(
        lambda seq_block: attend(*seq_block), (queries, key_rows, value_rows)
    )
    mixed_rows = attn_mix.reshape(flat_shape)
    attn_branch = lax.psum_scatter(
        jnp.dot(mixed_rows, out_weight, preferred_element_type=jnp.float32),
        "tensor",
        scatter_dimension=0,
        tiled=True,
    )
    hidden_res = residual + attn_branch
    normed_two, inv_two = normalize(hidden_res)
    ln_two = (normed_two * mlp_full.astype(jnp.float32)).astype(jnp.bfloat16)
    rows_two = lax.all_gather(ln_two, "tensor", axis=0, tiled=True)
    up_gate = jnp.einsum("td,idf->itf", rows_two, in_weight, preferred_element_type=jnp.float32)
    activated, gelu_slope = gelu_pair(up_gate[0])
    gate_part = up_gate[1]
    hidden_act = (activated * gate_part).astype(jnp.bfloat16)
    mlp_branch = lax.psum_scatter(
        jnp.dot(hidden_act, down_weight, preferred_element_type=jnp.float32).astype(jnp.bfloat16),
        "tensor",
        scatter_dimension=0,
        tiled=True,
    ).astype(jnp.float32)
    output = (hidden_res + mlp_branch).astype(jnp.bfloat16)
    grad_rows = lax.all_gather(cotangent, "tensor", axis=0, tiled=True)
    grad_down = jnp.einsum("tf,td->fd", hidden_act, grad_rows, preferred_element_type=jnp.float32)
    grad_act = jnp.einsum("td,fd->tf", grad_rows, down_weight, preferred_element_type=jnp.float32)
    grad_input_part = (grad_act * gate_part * gelu_slope).astype(jnp.bfloat16)
    grad_gate_part = (grad_act * activated).astype(jnp.bfloat16)
    grad_up_gate = jnp.stack([grad_input_part, grad_gate_part])
    grad_in = jnp.einsum("td,itf->idf", rows_two, grad_up_gate, preferred_element_type=jnp.float32)
    grad_ln_two = lax.psum_scatter(
        jnp.einsum("itf,idf->td", grad_up_gate, in_weight, preferred_element_type=jnp.float32),
        "tensor",
        scatter_dimension=0,
        tiled=True,
    )
    grad_res_two, mlp_gain_part = normalize_back(
        grad_ln_two, normed_two, inv_two, mlp_full.astype(jnp.float32)
    )
    grad_hidden = cotangent.astype(jnp.float32) + grad_res_two
    grad_hidden_rows = lax.all_gather(
        grad_hidden.astype(jnp.bfloat16), "tensor", axis=0, tiled=True
    )
    grad_out = jnp.einsum(
        "te,td->ed", mixed_rows, grad_hidden_rows, preferred_element_type=jnp.float32
    )
    grad_mix = (
        jnp.einsum("td,ed->te", grad_hidden_rows, out_weight, preferred_element_type=jnp.float32)
        .astype(jnp.bfloat16)
        .reshape(seq_shape)
    )
    grad_q, grad_k, grad_v = lax.map(
        lambda seq_block: attend_back(*seq_block),
        (queries, key_rows, value_rows, attn_mix, grad_mix, log_total),
    )
    grad_proj = jnp.stack(
        [
            rotate_back(grad_q.reshape(head_shape), cos_table, sin_table).reshape(flat_shape),
            rotate_back(grad_k.reshape(head_shape), cos_table, sin_table).reshape(flat_shape),
            grad_v.reshape(flat_shape),
        ]
    ).astype(jnp.bfloat16)
    grad_qkv = jnp.einsum("td,ite->ide", rows_one, grad_proj, preferred_element_type=jnp.float32)
    grad_ln_one = lax.psum_scatter(
        jnp.einsum("ite,ide->td", grad_proj, qkv_weight, preferred_element_type=jnp.float32),
        "tensor",
        scatter_dimension=0,
        tiled=True,
    )
    grad_res_one, attn_gain_part = normalize_back(
        grad_ln_one, normed_one, inv_one, attn_full.astype(jnp.float32)
    )
    input_grad = grad_hidden + grad_res_one
    reduced = (
        lax.psum_scatter(attn_gain_part, "dp", scatter_dimension=0, tiled=True),
        lax.psum_scatter(mlp_gain_part, "dp", scatter_dimension=0, tiled=True),
        lax.psum_scatter(grad_qkv, "dp", scatter_dimension=1, tiled=True),
        lax.psum_scatter(grad_out, "dp", scatter_dimension=1, tiled=True),
        lax.psum_scatter(grad_in, "dp", scatter_dimension=1, tiled=True),
        lax.psum_scatter(grad_down, "dp", scatter_dimension=1, tiled=True),
    )
    gain_attn, gain_mlp = lax.psum((reduced[0], reduced[1]), "tensor")
    return (output, input_grad, gain_attn, reduced[2], reduced[3], gain_mlp, reduced[4], reduced[5])


def solution(mesh):
    in_specs = (
        P(("dp", "tensor"), None),
        P("dp"),
        P(None, "dp", "tensor"),
        P("tensor", "dp"),
        P("dp"),
        P(None, "dp", "tensor"),
        P("tensor", "dp"),
        P(("dp", "tensor"), None),
    )
    out_specs = (
        P(("dp", "tensor"), None),
        P(("dp", "tensor"), None),
        P("dp"),
        P(None, "dp", "tensor"),
        P("tensor", "dp"),
        P("dp"),
        P(None, "dp", "tensor"),
        P("tensor", "dp"),
    )
    return jax.shard_map(body, mesh=mesh, in_specs=in_specs, out_specs=out_specs, check_vma=False)
```

profile of v0, /device:TPU:0, one launch (start us, length us, event | category | flops | bytes accessed | tf_op | source)
XLA Modules:
  0.0 582.5 jit_solution(6442852864527523916)
XLA Ops:
  13.1 23.1 %all-reduce.6 = (bf16[768]{0:T(1024)(128)(2,1)S(1)}, bf16[768]{0:T(1024)(128)(2,1)S(1)}) all-reduce(bf16[768]{0:T(1024)(128)(2,1)S(1)} %dynamic-update-slice, bf16[768]{0:T(1024)(128)(2,1)S(1)} %dynamic-update-slice.1), channel_id=1, replica_groups=mesh['dp'=8,'tensor'=4] {'dp'}, use_global_device_ids=true, to_apply=%add | all-reduce | flops 1536 | bytes 6144
  38.4 9.1 %all_gather.31 = bf16[512,768]{1,0:T(8,128)(2,1)} all-gather(bf16[128,768]{1,0:T(8,128)(2,1)S(1)} %fusion.19), channel_id=1, replica_groups=mesh['dp'=8,'tensor'=4] {'tensor'}, dimensions={0}, use_global_device_ids=true | all-gather | bytes 983040 | tf_op jit(solution)/shard_map/all_gather | solution.py:115
  47.5 36.2 %all_gather.32 = bf16[3,768,192]{2,0,1:T(4,128)(2,1)S(1)} all-gather(bf16[3,96,192]{2,0,1:T(4,128)(2,1)S(1)} %copy.27), channel_id=1, replica_groups=mesh['dp'=8,'tensor'=4] {'dp'}, dimensions={1}, use_global_device_ids=true | all-gather | bytes 995328 | tf_op jit(solution)/shard_map/all_gather | solution.py:104
  86.9 31.0 %all_gather.33 = bf16[192,768]{0,1:T(8,128)(2,1)S(1)} all-gather(bf16[192,96]{0,1:T(8,128)(2,1)S(1)} %copy.30), channel_id=1, replica_groups=mesh['dp'=8,'tensor'=4] {'dp'}, dimensions={1}, use_global_device_ids=true | all-gather | bytes 331776 | tf_op jit(solution)/shard_map/all_gather | solution.py:105
  124.7 33.5 %all_gather.37 = bf16[288,768]{0,1:T(8,128)(2,1)} all-gather(bf16[288,96]{0,1:T(8,128)(2,1)S(1)} %copy.33), channel_id=1, replica_groups=mesh['dp'=8,'tensor'=4] {'dp'}, dimensions={1}, use_global_device_ids=true | all-gather | bytes 497664 | tf_op jit(solution)/shard_map/all_gather | solution.py:110
  158.3 8.1 %all_gather.38 = bf16[512,768]{1,0:T(8,128)(2,1)} all-gather(bf16[128,768]{1,0:T(8,128)(2,1)S(1)} %copy-done.21), channel_id=1, replica_groups=mesh['dp'=8,'tensor'=4] {'tensor'}, dimensions={0}, use_global_device_ids=true | all-gather | bytes 983040 | tf_op jit(solution)/shard_map/all_gather | solution.py:159
  166.3 35.4 %all_gather.36 = bf16[2,768,288]{2,0,1:T(2,128)(2,1)} all-gather(bf16[2,96,288]{2,0,1:T(2,128)(2,1)S(1)} %copy.31), channel_id=1, replica_groups=mesh['dp'=8,'tensor'=4] {'dp'}, dimensions={1}, use_global_device_ids=true | all-gather | bytes 995328 | tf_op jit(solution)/shard_map/all_gather | solution.py:109
  203.8 8.6 %all_gather.35 = bf16[512,768]{1,0:T(8,128)(2,1)S(1)} all-gather(bf16[128,768]{1,0:T(8,128)(2,1)S(1)} %multiply_convert_fusion.3), channel_id=1, replica_groups=mesh['dp'=8,'tensor'=4] {'tensor'}, dimensions={0}, use_global_device_ids=true | all-gather | bytes 983040 | tf_op jit(solution)/shard_map/all_gather | solution.py:147
  221.1 3.0 convolution_bitcast_fusion.5
  224.1 3.2 convolution_bitcast_fusion
  227.3 5.2 copy.51
  232.5 3.9 reshape.180
  236.6 7.5 %reduce-scatter.21.cloned.1.call-done = f32[128,768]{1,0:T(8,128)} async-done(((f32[512,768]{1,0:T(8,128)}), f32[128,768]{1,0:T(8,128)}) %reduce-scatter.21.cloned.1.call-update) | async-done | bytes 393232 | tf_op jit(solution)/shard_map/reduce_scatter | solution.py:166
  247.0 22.9 %reduce-scatter.19.cloned.1.call-done = bf16[128,768]{1,0:T(8,128)(2,1)} async-done(((bf16[512,768]{1,0:T(8,128)(2,1)}), bf16[128,768]{1,0:T(8,128)(2,1)}) %reduce-scatter.19.cloned.1.call-update) | async-done | bytes 196624 | tf_op jit(solution)/shard_map/reduce_scatter | solution.py:152
  272.1 8.0 %all_gather.39 = bf16[512,768]{1,0:T(8,128)(2,1)S(1)} all-gather(bf16[128,768]{1,0:T(8,128)(2,1)S(1)} %get-tuple-element.84), channel_id=1, replica_groups=mesh['dp'=8,'tensor'=4] {'tensor'}, dimensions={0}, use_global_device_ids=true | all-gather | bytes 983040 | tf_op jit(solution)/shard_map/all_gather | solution.py:176
  292.4 2.9 convolution_bitcast_fusion.1
  295.3 3.0 copy.47
  301.8 35.9 %reduce-scatter.31.cloned.1.call-done = f32[96,288]{1,0:T(8,128)} async-done(((f32[768,288]{1,0:T(8,128)}), f32[96,288]{1,0:T(8,128)}) %reduce-scatter.31.cloned.1.call-update) | async-done | bytes 110608
  339.4 68.1 %reduce-scatter.29.cloned.1.call-done = f32[96,576]{1,0:T(8,128)} async-done(((f32[768,576]{1,0:T(8,128)}), f32[96,576]{1,0:T(8,128)}) %reduce-scatter.29.cloned.1.call-update) | async-done | bytes 221200
  409.5 63.5 %reduce-scatter.27.cloned.1.call-done = f32[96,192]{1,0:T(8,128)} async-done(((f32[768,192]{1,0:T(8,128)}), f32[96,192]{1,0:T(8,128)}) %reduce-scatter.27.cloned.1.call-update) | async-done | bytes 73744
  474.6 27.9 %reduce-scatter.23.cloned.1.call-done = f32[128,768]{1,0:T(8,128)} async-done(((f32[512,768]{1,0:T(8,128)}), f32[128,768]{1,0:T(8,128)}) %reduce-scatter.23.cloned.1.call-update) | async-done | bytes 393232 | tf_op jit(solution)/shard_map/reduce_scatter | solution.py:199
  503.8 21.8 %all-reduce.4 = (f32[768]{0:T(1024)S(1)}, f32[768]{0:T(1024)S(1)}) all-reduce(f32[768]{0:T(1024)S(1)} %get-tuple-element.74, f32[768]{0:T(1024)S(1)} %copy-done.29), channel_id=6, replica_groups=mesh['dp'=8,'tensor'=4] {'dp'}, use_global_device_ids=true, to_apply=%region_16.17.clone | all-reduce | flops 1536 | bytes 12288
  525.8 6.6 %all-reduce.5 = (f32[96]{0:T(128)}, f32[96]{0:T(128)}) all-reduce(f32[96]{0:T(128)S(1)} %dynamic-slice.7, f32[96]{0:T(128)S(1)} %dynamic-slice.9), channel_id=1, replica_groups=mesh['dp'=8,'tensor'=4] {'tensor'}, use_global_device_ids=true, to_apply=%region_17.18 | all-reduce | flops 192 | bytes 1536 | tf_op jit(solution)/shard_map/psum | solution.py:217
  534.3 39.4 %reduce-scatter.25.cloned.1.call-done = f32[96,576]{1,0:T(8,128)} async-done(((f32[768,576]{1,0:T(8,128)}), f32[96,576]{1,0:T(8,128)}) %reduce-scatter.25.cloned.1.call-update) | async-done | bytes 221200
  (157 shorter events, 58.7 us)
Async XLA Ops:
  7.2 194.6 %reduce-scatter.17.cloned.1.call-start = ((), (), s32[]{:S(2)}) async-start(), calls=%async_computation.8 | async-start | bytes 1966080 | tf_op jit(solution)/shard_map/reduce_scatter | solution.py:138
  8.3 75.4 %copy-start.30 = (f32[128]{0:T(128)}, f32[128]{0:T(128)S(1)}, u32[]{:S(2)}) copy-start(f32[128]{0:T(128)S(1)} %broadcast_multiply_fusion.10) | copy-start | bytes 1540
  9.4 74.2 %copy-start.33 = (f32[128]{0:T(128)}, f32[128]{0:T(128)S(1)}, u32[]{:S(2)}) copy-start(f32[128]{0:T(128)S(1)} %add_rsqrt_fusion.1) | copy-start | bytes 1540
  86.8 33.8 %copy-start.15 = (bf16[1,512,192]{1,2,0:T(8,128)(2,1)}, bf16[1,512,192]{1,2,0:T(8,128)(2,1)S(1)}, u32[]{:S(2)}) copy-start(bf16[1,512,192]{1,2,0:T(8,128)(2,1)S(1)} %slice.97) | copy-start | bytes 589828
  117.9 3.3 copy-start.6
  123.5 34.8 %copy-start.21 = (bf16[128,768]{1,0:T(8,128)(2,1)S(1)}, bf16[128,768]{1,0:T(8,128)(2,1)}, u32[]{:S(2)}) copy-start(bf16[128,768]{1,0:T(8,128)(2,1)} %param.15) | copy-start | bytes 589828
  123.5 120.6 %reduce-scatter.21.cloned.1.call-start = ((), (), s32[]{:S(2)}) async-start(), calls=%async_computation.10 | async-start | bytes 1966080 | tf_op jit(solution)/shard_map/reduce_scatter | solution.py:166
  201.8 10.6 %copy-start.3 = (bf16[2,768,288]{2,0,1:T(2,128)(2,1)S(1)}, bf16[2,768,288]{2,0,1:T(2,128)(2,1)}, u32[]{:S(2)}) copy-start(bf16[2,768,288]{2,0,1:T(2,128)(2,1)} %all_gather.36) | copy-start | bytes 2654212
  212.4 2.9 copy-start.1
  218.2 51.6 %reduce-scatter.19.cloned.1.call-start = ((), (), s32[]{:S(2)}) async-start(), calls=%async_computation.9 | async-start | bytes 983040 | tf_op jit(solution)/shard_map/reduce_scatter | solution.py:152
  221.0 116.7 %reduce-scatter.31.cloned.1.call-start = ((), (), s32[]{:S(2)}) async-start(), calls=%async_computation.15 | async-start | bytes 1327104
  224.1 183.5 %reduce-scatter.29.cloned.1.call-start = ((), (), s32[]{:S(2)}) async-start(), calls=%async_computation.14 | async-start | bytes 2211840
  236.4 236.6 %reduce-scatter.27.cloned.1.call-start = ((), (), s32[]{:S(2)}) async-start(), calls=%async_computation.13 | async-start | bytes 884736
  269.9 10.2 %copy-start.7 = (bf16[192,768]{0,1:T(8,128)(2,1)S(1)}, bf16[192,768]{0,1:T(8,128)(2,1)}, u32[]{:S(2)}) copy-start(bf16[192,768]{0,1:T(8,128)(2,1)} %copy-done.6) | copy-start | bytes 884740
  269.9 10.7 %copy-start.11 = (bf16[3,64,512]{2,1,0:T(8,128)(2,1)S(1)}, bf16[3,64,512]{2,1,0:T(8,128)(2,1)}, u32[]{:S(2)}) copy-start(bf16[3,64,512]{2,1,0:T(8,128)(2,1)} %copy-done.10) | copy-start | bytes 589828
  280.1 2.6 copy-start.16
  282.6 2.8 copy-start.18
  286.0 216.6 %reduce-scatter.23.cloned.1.call-start = ((), (), s32[]{:S(2)}) async-start(), calls=%async_computation.11 | async-start | bytes 1966080 | tf_op jit(solution)/shard_map/reduce_scatter | solution.py:199
  292.3 281.5 %reduce-scatter.25.cloned.1.call-start = ((), (), s32[]{:S(2)}) async-start(), calls=%async_computation.12 | async-start | bytes 2211840
  301.1 201.5 %copy-start.2 = (bf16[128,768]{1,0:T(8,128)(2,1)S(1)}, bf16[128,768]{1,0:T(8,128)(2,1)}, u32[]{:S(2)}) copy-start(bf16[128,768]{1,0:T(8,128)(2,1)} %param.8) | copy-start | bytes 589828
  301.1 201.5 %copy-start.31 = (f32[128]{0:T(128)S(1)}, f32[128]{0:T(128)}, u32[]{:S(2)}) copy-start(f32[128]{0:T(128)} %copy-done.30) | copy-start | bytes 1540
  301.1 201.5 %copy-start.34 = (f32[128]{0:T(128)S(1)}, f32[128]{0:T(128)}, u32[]{:S(2)}) copy-start(f32[128]{0:T(128)} %copy-done.33) | copy-start | bytes 1540
  301.1 202.8 %copy-start.29 = (f32[768]{0:T(1024)S(1)}, f32[768]{0:T(1024)}, u32[]{:S(2)}) copy-start(f32[768]{0:T(1024)} %get-tuple-element.72) | copy-start | bytes 9220
  301.1 231.3 %copy-start.20 = (f32[128,768]{1,0:T(8,128)S(1)}, f32[128,768]{1,0:T(8,128)}, u32[]{:S(2)}) copy-start(f32[128,768]{1,0:T(8,128)} %get-tuple-element.85) | copy-start | bytes 1179652
  (20 other events, 24.9 us)
Sparse Core Ops, SparseCore 0:
  123.6 26.1 reduce-scatter.16
  218.4 25.6 reduce-scatter.20
  246.6 23.1 reduce-scatter.18
  273.1 64.6 reduce-scatter.30
  341.1 66.4 reduce-scatter.28
  410.7 62.2 reduce-scatter.26
  475.5 27.0 reduce-scatter.22
  506.1 67.6 reduce-scatter.24
where the time goes:
time: 584 us; the launch traced here: 582 us
  waiting for transfers between devices  265 us (45%)
  blocking collectives  221 us (38%)
  local copies, waits for them, and re-layouts  33.7 us (6%)
  matrix products  29.5 us (5%)
  between operations  16 us (3%)
  other arithmetic  15.9 us (3%)
    unnamed x12, waiting for transfers between devices  207 us
    unnamed x2, blocking collectives  44.9 us
    all_gather x1, blocking collectives, body(): lax.all_gather(w_qkv, 'dp', axis=1, tiled=True)  36.2 us
    all_gather x1, blocking collectives, body(): lax.all_gather(w_in, 'dp', axis=1, tiled=True)  35.4 us
    all_gather x1, blocking collectives, body(): lax.all_gather(w_down, 'dp', axis=1, tiled=True)  33.5 us
    unnamed x93, local copies, waits for them, and re-layouts  32.8 us
    all_gather x1, blocking collectives, body(): lax.all_gather(w_out, 'dp', axis=1, tiled=True)  31 us
    reduce_scatter x1, waiting for transfers between devices, body(): lax.psum_scatter(jnp.einsum('ite,ide->td', grad_proj, qkv_weight, preferr...  27.9 us
  transfers between devices with their start and end apart: 8, of which 7 were waited for; matrix products, arithmetic and copies ran while one was open for 9% of the time, Pallas kernels for 0%

commit v1 on v0

v1 whole, which is shorter than its diff:
```python
import functools

import jax
import jax.numpy as jnp
from jax import lax
from jax.experimental import pallas as pl
from jax.experimental.pallas import tpu as pltpu
from jax.sharding import PartitionSpec as P

HD = 64
L = 512


NORM_EPS = 1e-05
ROPE_THETA = 160000.0
SQRT_HALF = 0.7071067811865476
GAUSS_NORM = 0.3989422804014327


def rope_tables(row_count):
    position = (jnp.arange(row_count) % L).astype(jnp.float32)
    halves = jnp.arange(HD // 2).astype(jnp.float32)
    inverse = ROPE_THETA ** (-2.0 * halves / HD)
    angles = position[:, None] * inverse[None, :]
    angles = jnp.concatenate([angles, angles], axis=1)
    return (jnp.cos(angles)[:, None, :], jnp.sin(angles)[:, None, :])


def rotate(field_rows, cos_table, sin_table):
    first_half = field_rows[..., : HD // 2]
    second_half = field_rows[..., HD // 2 :]
    turned = jnp.concatenate([-second_half, first_half], axis=-1)
    return field_rows * cos_table + turned * sin_table


def rotate_back(grad_field, cos_table, sin_table):
    scaled = grad_field * sin_table
    turned = jnp.concatenate([scaled[..., HD // 2 :], -scaled[..., : HD // 2]], axis=-1)
    return grad_field * cos_table + turned


def normalize(values):
    centred = values - jnp.mean(values, axis=-1, keepdims=True)
    inv_std = lax.rsqrt(jnp.mean(centred * centred, axis=-1, keepdims=True) + NORM_EPS)
    return (centred * inv_std, inv_std)


def normalize_back(grad_norm, normed, inv_std, gain_row):
    gain_part = jnp.sum(grad_norm * normed, axis=0)
    scaled = grad_norm * gain_row
    centred = scaled - jnp.mean(scaled, axis=-1, keepdims=True)
    grad_in = inv_std * (centred - normed * jnp.mean(scaled * normed, axis=-1, keepdims=True))
    return (grad_in, gain_part)


def gelu_pair(inputs):
    normal_cdf = 0.5 * (1.0 + lax.erf(inputs * SQRT_HALF))
    return (inputs * normal_cdf, normal_cdf + inputs * jnp.exp(-0.5 * inputs * inputs) * GAUSS_NORM)


def attend(queries, key_rows, value_rows):
    score_scale = HD ** (-0.5)
    scores = (
        jnp.einsum("qhd,khd->hqk", queries, key_rows, preferred_element_type=jnp.float32)
        * score_scale
    )
    row_max = jnp.max(scores, axis=-1, keepdims=True)
    log_total = row_max + jnp.log(jnp.sum(jnp.exp(scores - row_max), axis=-1, keepdims=True))
    weights = jnp.exp(scores - log_total).astype(jnp.bfloat16)
    attn_mix = jnp.einsum(
        "hqk,khd->qhd", weights, value_rows, preferred_element_type=jnp.float32
    ).astype(jnp.bfloat16)
    return (attn_mix, log_total)


def attend_back(queries, key_rows, value_rows, attn_mix, grad_mix, log_total):
    score_scale = HD ** (-0.5)
    scores = (
        jnp.einsum("qhd,khd->hqk", queries, key_rows, preferred_element_type=jnp.float32)
        * score_scale
    )
    probabilities = jnp.exp(scores - log_total)
    grad_probs = jnp.einsum(
        "qhd,khd->hqk", grad_mix, value_rows, preferred_element_type=jnp.float32
    )
    row_delta = jnp.sum(grad_mix.astype(jnp.float32) * attn_mix.astype(jnp.float32), axis=-1)
    grad_scores = (probabilities * (grad_probs - jnp.transpose(row_delta)[:, :, None])).astype(
        jnp.bfloat16
    )
    prob_rounded = probabilities.astype(jnp.bfloat16)
    grad_values = jnp.einsum(
        "hqk,qhd->khd", prob_rounded, grad_mix, preferred_element_type=jnp.float32
    )
    grad_queries = (
        jnp.einsum("hqk,khd->qhd", grad_scores, key_rows, preferred_element_type=jnp.float32)
        * score_scale
    )
    grad_keys = (
        jnp.einsum("hqk,qhd->khd", grad_scores, queries, preferred_element_type=jnp.float32)
        * score_scale
    )
    return (grad_queries, grad_keys, grad_values)


def exchange_kernel(plan, sizes, *refs):
    count = len(plan)
    sources, targets = refs[:count], refs[count : 2 * count]
    own_sem, send_sem, recv_sem = refs[2 * count :]
    axes = sorted({axis for _, axis in plan})
    barrier = pltpu.get_barrier_semaphore()
    total = 0
    for axis in axes:
        me = lax.axis_index(axis)
        for shift in range(1, sizes[axis]):
            pl.semaphore_signal(
                barrier,
                inc=1,
                device_id={axis: lax.rem(me + shift, sizes[axis])},
                device_id_type=pl.DeviceIdType.MESH,
            )
            total += 1
    pl.semaphore_wait(barrier, total)
    slot = 0
    pending, relays, local = [], [], []

    def remote(source, target, axis, peer, index):
        return pltpu.make_async_remote_copy(
            src_ref=source,
            dst_ref=target,
            send_sem=send_sem.at[index],
            recv_sem=recv_sem.at[index],
            device_id={axis: peer},
            device_id_type=pl.DeviceIdType.MESH,
        )

    for which, (kind, axis) in enumerate(plan):
        size = sizes[axis]
        me = lax.axis_index(axis)
        source, target = sources[which], targets[which]
        if kind == "relay":
            outer = size // 2
            column = lax.rem(me, 2)
            row = me // 2
            partner = row * 2 + 1 - column
            for shift in range(1, outer):
                peer = lax.rem(row + shift, outer) * 2 + column
                copy = remote(source, target.at[me], axis, peer, slot)
                copy.start()
                origin = lax.rem(row + outer - shift, outer) * 2 + column
                relays.append((copy, target, axis, origin, partner, slot + 1))
                slot += 2
            copy = remote(source, target.at[me], axis, partner, slot)
            copy.start()
            pending.append(copy)
            slot += 1
        else:
            for shift in range(1, size):
                peer = lax.rem(me + shift, size)
                piece = source if kind == "gather" else source.at[peer]
                copy = remote(piece, target.at[me], axis, peer, slot)
                copy.start()
                pending.append(copy)
                slot += 1
        piece = source if kind != "scatter" else source.at[me]
        copy = pltpu.make_async_copy(piece, target.at[me], own_sem.at[which])
        copy.start()
        local.append(copy)
    for copy, target, axis, origin, partner, index in relays:
        copy.wait_recv()
        onward = remote(target.at[origin], target.at[origin], axis, partner, index)
        onward.start()
        pending.append(onward)
    for copy, *_ in relays:
        copy.wait_send()
    for copy in pending + local:
        copy.wait()


def slots_of(kind, size):
    return 2 * (size // 2 - 1) + 1 if kind == "relay" else size - 1


def exchange(sizes, number, *ops):
    plan = tuple((kind, axis) for kind, axis, _ in ops)
    arrays = [array for _, _, array in ops]
    shapes = [
        jax.ShapeDtypeStruct(
            array.shape if kind == "scatter" else (sizes[axis],) + array.shape, array.dtype
        )
        for kind, axis, array in ops
    ]
    slots = sum(slots_of(kind, sizes[axis]) for kind, axis in plan)
    return pl.pallas_call(
        functools.partial(exchange_kernel, plan, sizes),
        out_shape=shapes,
        in_specs=[pl.BlockSpec(memory_space=pltpu.VMEM)] * len(arrays),
        out_specs=[pl.BlockSpec(memory_space=pltpu.VMEM)] * len(arrays),
        scratch_shapes=[
            pltpu.SemaphoreType.DMA((len(arrays),)),
            pltpu.SemaphoreType.DMA((slots,)),
            pltpu.SemaphoreType.DMA((slots,)),
        ],
        compiler_params=pltpu.CompilerParams(
            collective_id=number, has_side_effects=True, vmem_limit_bytes=48 << 20
        ),
    )(*arrays)


def pad_columns(array, multiple=128):
    extra = -array.shape[-1] % multiple
    return jnp.pad(array, [(0, 0)] * (array.ndim - 1) + [(0, extra)])


def total_of(pieces):
    return jnp.sum(pieces.astype(jnp.float32), axis=0)


def dot_f32(left, right, left_dim, right_dim):
    return lax.dot_general(
        left, right, (((left_dim,), (right_dim,)), ((), ())), preferred_element_type=jnp.float32
    )


def body(sizes, tokens, attn_gain, w_qkv, w_out, mlp_gain, w_in, w_down, cotangent):
    bf16, f32 = jnp.bfloat16, jnp.float32
    groups, members = sizes["dp"], sizes["tensor"]
    block = w_qkv.shape[1]
    width = block * groups
    heads_wide, hidden = w_qkv.shape[2], w_in.shape[2]
    own_rows = tokens.shape[0]
    packed = pad_columns(
        jnp.concatenate(
            [w_qkv[0], w_qkv[1], w_qkv[2], w_out.T, w_in[0], w_in[1], w_down.T]
            + [attn_gain[:, None], mlp_gain[:, None]],
            axis=1,
        )
    )
    weights, token_rows, grad_rows = exchange(
        sizes,
        0,
        ("relay", "dp", packed),
        ("gather", "tensor", tokens),
        ("gather", "tensor", cotangent),
    )
    weights = weights.reshape(width, -1)
    edges = [3 * heads_wide, 4 * heads_wide, 4 * heads_wide + 2 * hidden, 4 * heads_wide + 3 * hidden]
    qkv_weight = weights[:, : edges[0]]
    out_weight_t = weights[:, edges[0] : edges[1]]
    in_weight = weights[:, edges[1] : edges[2]]
    down_weight_t = weights[:, edges[2] : edges[3]]
    gains = weights[:, edges[3] : edges[3] + 2].astype(f32).T
    attn_full, mlp_full = gains[0:1], gains[1:2]
    row_count = own_rows * members
    grad_rows = grad_rows.reshape(row_count, width)
    residual = tokens.astype(f32)
    normed_one, inv_one = normalize(residual)
    rows_one = (normalize(token_rows.reshape(row_count, width).astype(f32))[0] * attn_full).astype(bf16)
    head_count = heads_wide // HD
    head_shape = (row_count, head_count, HD)
    seq_shape = (row_count // L, L, head_count, HD)
    flat_shape = (row_count, heads_wide)
    cos_table, sin_table = rope_tables(row_count)
    projected = dot_f32(rows_one, qkv_weight, 1, 0)
    pieces = [projected[:, i * heads_wide : (i + 1) * heads_wide].reshape(head_shape) for i in range(3)]
    queries = rotate(pieces[0], cos_table, sin_table).astype(bf16).reshape(seq_shape)
    key_rows = rotate(pieces[1], cos_table, sin_table).astype(bf16).reshape(seq_shape)
    value_rows = pieces[2].astype(bf16).reshape(seq_shape)
    one_seq = row_count == L

    def over_sequences(function, arrays):
        if one_seq:
            results = function(*[array[0] for array in arrays])
            return tuple(result[None] for result in results)
        return lax.map(lambda seq_block: function(*seq_block), arrays)

    attn_mix, log_total = over_sequences(attend, (queries, key_rows, value_rows))
    mixed_rows = attn_mix.reshape(flat_shape)
    attn_part = dot_f32(mixed_rows, out_weight_t, 1, 1).astype(bf16)
    (attn_parts,) = exchange(
        sizes, 1, ("scatter", "tensor", attn_part.reshape(members, own_rows, width))
    )
    hidden_res = residual + total_of(attn_parts)
    normed_two, inv_two = normalize(hidden_res)
    ln_two = (normed_two * mlp_full).astype(bf16)
    (rows_two,) = exchange(sizes, 2, ("gather", "tensor", ln_two))
    rows_two = rows_two.reshape(row_count, width)
    up_gate = dot_f32(rows_two, in_weight, 1, 0)
    activated, gelu_slope = gelu_pair(up_gate[:, :hidden])
    gate_part = up_gate[:, hidden:]
    hidden_act = (activated * gate_part).astype(bf16)
    mlp_part = dot_f32(hidden_act, down_weight_t, 1, 1).astype(bf16)
    grad_down_t = dot_f32(grad_rows, hidden_act, 0, 0).astype(bf16)
    grad_act = dot_f32(grad_rows, down_weight_t, 1, 0)
    grad_up_gate = jnp.concatenate(
        [(grad_act * gate_part * gelu_slope).astype(bf16), (grad_act * activated).astype(bf16)], axis=1
    )
    grad_in = dot_f32(rows_two, grad_up_gate, 0, 0).astype(bf16)
    ln_two_part = dot_f32(grad_up_gate, in_weight, 1, 1).astype(bf16)
    mlp_parts, ln_two_parts, grad_down_parts = exchange(
        sizes,
        3,
        ("scatter", "tensor", mlp_part.reshape(members, own_rows, width)),
        ("scatter", "tensor", ln_two_part.reshape(members, own_rows, width)),
        ("scatter", "dp", pad_columns(grad_down_t).reshape(groups, block, -1)),
    )
    output = (hidden_res + total_of(mlp_parts)).astype(bf16)
    grad_res_two, mlp_gain_part = normalize_back(total_of(ln_two_parts), normed_two, inv_two, mlp_full)
    grad_hidden = cotangent.astype(f32) + grad_res_two
    half = hidden
    grad_hidden_rows, grad_in_parts_a = exchange(
        sizes,
        4,
        ("gather", "tensor", grad_hidden.astype(bf16)),
        ("scatter", "dp", pad_columns(grad_in[:, :half]).reshape(groups, block, -1)),
    )
    grad_hidden_rows = grad_hidden_rows.reshape(row_count, width)
    grad_out_t = dot_f32(grad_hidden_rows, mixed_rows, 0, 0).astype(bf16)
    grad_mix = dot_f32(grad_hidden_rows, out_weight_t, 1, 0).astype(bf16).reshape(seq_shape)
    grad_q, grad_k, grad_v = over_sequences(
        attend_back, (queries, key_rows, value_rows, attn_mix, grad_mix, log_total)
    )
    grad_proj = jnp.concatenate(
        [
            rotate_back(grad_q.reshape(head_shape), cos_table, sin_table).reshape(flat_shape),
            rotate_back(grad_k.reshape(head_shape), cos_table, sin_table).reshape(flat_shape),
            grad_v.reshape(flat_shape),
        ],
        axis=1,
    ).astype(bf16)
    grad_qkv = dot_f32(rows_one, grad_proj, 0, 0).astype(bf16)
    ln_one_part = dot_f32(grad_proj, qkv_weight, 1, 1).astype(bf16)
    ln_one_parts, grad_in_parts_b = exchange(
        sizes,
        5,
        ("scatter", "tensor", ln_one_part.reshape(members, own_rows, width)),
        ("scatter", "dp", pad_columns(grad_in[:, half:]).reshape(groups, block, -1)),
    )
    grad_res_one, attn_gain_part = normalize_back(total_of(ln_one_parts), normed_one, inv_one, attn_full)
    input_grad = grad_hidden + grad_res_one
    gain_parts = jnp.stack([attn_gain_part, mlp_gain_part] + [jnp.zeros_like(attn_gain_part)] * 6)
    gain_parts = pad_columns(jnp.swapaxes(gain_parts.reshape(8, groups, block), 0, 1))
    late_parts, gain_parts = exchange(
        sizes,
        6,
        ("scatter", "dp", jnp.concatenate([grad_qkv, grad_out_t], axis=1).reshape(groups, block, -1)),
        ("scatter", "dp", gain_parts),
    )
    (gain_groups,) = exchange(sizes, 7, ("gather", "tensor", total_of(gain_parts)))
    gain_sum = total_of(gain_groups)
    late = total_of(late_parts)
    grad_w_qkv = jnp.stack([late[:, i * heads_wide : (i + 1) * heads_wide] for i in range(3)])
    grad_w_out = late[:, 3 * heads_wide : 4 * heads_wide].T
    grad_w_in = jnp.stack([total_of(grad_in_parts_a)[:, :hidden], total_of(grad_in_parts_b)[:, :hidden]])
    grad_w_down = total_of(grad_down_parts)[:, :hidden].T
    return (
        output,
        input_grad,
        gain_sum[0, :block],
        grad_w_qkv,
        grad_w_out,
        gain_sum[1, :block],
        grad_w_in,
        grad_w_down,
    )


def solution(mesh):
    in_specs = (
        P(("dp", "tensor"), None),
        P("dp"),
        P(None, "dp", "tensor"),
        P("tensor", "dp"),
        P("dp"),
        P(None, "dp", "tensor"),
        P("tensor", "dp"),
        P(("dp", "tensor"), None),
    )
    out_specs = (
        P(("dp", "tensor"), None),
        P(("dp", "tensor"), None),
        P("dp"),
        P(None, "dp", "tensor"),
        P("tensor", "dp"),
        P("dp"),
        P(None, "dp", "tensor"),
        P("tensor", "dp"),
    )
    sizes = {axis: mesh.shape[axis] for axis in ("dp", "tensor")}
    return jax.shard_map(functools.partial(body, sizes), mesh=mesh, in_specs=in_specs, out_specs=out_specs, check_vma=False)
```

time: 584 us -> 233 us (0.40)
  waiting for transfers between devices: 265 us -> 0 us
  blocking collectives: 221 us -> 0 us
  Pallas kernels: 0 us -> 159 us
  between operations: 16 us -> 1.35 us
  matrix products: 29.5 us -> 16.3 us
  other arithmetic: 15.9 us -> 22.3 us
    unnamed x12 -> x0, waiting for transfers between devices: 207 us -> none
    all_gather x8 -> x0, blocking collectives: 170 us -> none  [the longest x1 36.2 us: body(): lax.all_gather(w_qkv, 'dp', axis=1, tiled=True)]
    pallas_call x0 -> x8, Pallas kernels: none -> 159 us  [exchange(): pl.pallas_call(functools.partial(exchange_kernel, plan, sizes), out_shape...]
    reduce_scatter x4 -> x0, waiting for transfers between devices: 58.3 us -> none  [the longest x1 27.9 us: body(): lax.psum_scatter(jnp.einsum('ite,ide->td', grad_proj, qkv_weight, preferr...]
    unnamed x2 -> x0, blocking collectives: 44.9 us -> none
    unnamed x93, local copies, waits for them, and re-layouts: 32.8 us -> 17.2 us
    psum x1 -> x0, blocking collectives: 6.57 us -> none  [body(): gain_attn, gain_mlp = lax.psum((reduced[0], reduced[1]), 'tensor')]
    unnamed x3 -> x0, matrix products: 6.5 us -> none
  transfers between devices with their start and end apart: 8 -> 0, of which waited for: 7 -> 0; matrix products, arithmetic and copies ran while one was open for 9% -> 0% of each run, Pallas kernels for 0% -> 0%
where the time goes in v1:
time: 233 us; the launch traced here: 232 us
  Pallas kernels  159 us (68%)
  local copies, waits for them, and re-layouts  32.3 us (14%)
  other arithmetic  22.3 us (10%)
  matrix products  16.3 us (7%)
    pallas_call x8, Pallas kernels, exchange(): pl.pallas_call(functools.partial(exchange_kernel, plan, sizes), out_shape...  159 us
    unnamed x93, local copies, waits for them, and re-layouts  17.2 us
    dot_general x12, matrix products, dot_f32(): lax.dot_general(left, right, (((left_dim,), (right_dim,)), ((), ())), pre...  12.5 us

profile of v1, /device:TPU:0, one launch (start us, length us, event | category | flops | bytes accessed | tf_op | source)
XLA Modules:
  0.0 231.5 jit_solution(8345585498098275808)
XLA Ops:
  11.1 42.9 %shard_map.143 = (bf16[8,96,1664]{2,1,0:T(8,128)(2,1)S(1)}, bf16[4,128,768]{2,1,0:T(8,128)(2,1)S(1)}, bf16[4,128,768]{2,1,0:T(8,128)(2,1)S(1)}) custom-call(bf16[96,1664]{1,0:T(8,128)(2,1)S(1)} %pad.18.refs_0_, bf16[128,768]{1,0:T(8,128)(2,1)S(1)} %copy-done, bf16[128,768]{1,0:T(8,128)(2,1)S(1)} %copy-done.7), custom_call_target="tpu_custom_call" | custom-call | tf_op jit(solution)/shard_map/pallas_call | solution.py:193
  57.5 1.1 copy.69
  65.6 10.0 %shard_map.144 = bf16[4,128,768]{2,1,0:T(8,128)(2,1)S(1)} custom-call(bf16[4,128,768]{2,1,0:T(8,128)(2,1)S(1)} %bitcast.111), custom_call_target="tpu_custom_call" | custom-call | tf_op jit(solution)/shard_map/pallas_call | solution.py:193
  76.9 10.9 %shard_map.145 = bf16[4,128,768]{2,1,0:T(8,128)(2,1)S(1)} custom-call(bf16[128,768]{1,0:T(8,128)(2,1)S(1)} %multiply_convert_fusion.3.refs_0_), custom_call_target="tpu_custom_call" | custom-call | tf_op jit(solution)/shard_map/pallas_call | solution.py:193
  90.0 1.2 convolution_convert_fusion.6
  91.2 1.5 convolution_convert_fusion.1
  92.7 1.3 copy.67
  94.9 2.9 %convolution_convert_fusion.3 = bf16[512,768]{1,0:T(8,128)(2,1)} fusion(bf16[768,1664]{1,0:T(8,128)(2,1)S(1)} %bitcast.105, bf16[512,288]{0,1:T(8,128)(2,1)} %copy-done.42, bf16[512,288]{0,1:T(8,128)(2,1)} %copy-done.41), kind=kOutput, calls=%fused_computation.18 | convolution fusion | flops 454557696 | bytes 2359296 | tf_op jit(solution)/shard_map/dot_general | solution.py:219
  99.5 1.4 copy.52
  100.9 2.1 copy.68
  103.0 2.1 pad.21.clone
  105.0 1.7 convolution_convert_fusion.5
  106.8 27.6 %shard_map.146 = (bf16[4,128,768]{2,1,0:T(8,128)(2,1)S(1)}, bf16[4,128,768]{2,1,0:T(8,128)(2,1)S(1)}, bf16[8,96,384]{2,1,0:T(8,128)(2,1)S(1)}) custom-call(bf16[4,128,768]{2,1,0:T(8,128)(2,1)S(1)} %bitcast.120, bf16[4,128,768]{2,1,0:T(8,128)(2,1)S(1)} %bitcast.119, bf16[8,96,384]{2,1,0:T(8,128)(2,1)S(1)} %bitcast.116), custom_call_target="tpu_custom_call" | custom-call | tf_op jit(solution)/shard_map/pallas_call | solution.py:193
  136.9 1.7 copy.60
  138.6 2.0 convert_reduce_fusion.2
  140.6 1.9 multiply_reduce_fusion.2
  142.6 1.4 stack.37
  145.2 2.2 fusion.53
  147.4 13.8 %shard_map.147 = (bf16[4,128,768]{2,1,0:T(8,128)(2,1)S(1)}, bf16[8,96,384]{2,1,0:T(8,128)(2,1)S(1)}) custom-call(bf16[128,768]{1,0:T(8,128)(2,1)S(1)} %get-tuple-element.64.refs_0_, bf16[8,96,384]{2,1,0:T(8,128)(2,1)S(1)} %bitcast.114), custom_call_target="tpu_custom_call" | custom-call | tf_op jit(solution)/shard_map/pallas_call | solution.py:193
  169.4 1.1 pad_maximum_fusion
  170.5 1.6 copy.58
  172.2 16.7 %shard_map.148 = (bf16[4,128,768]{2,1,0:T(8,128)(2,1)S(1)}, bf16[8,96,384]{2,1,0:T(8,128)(2,1)S(1)}) custom-call(bf16[4,128,768]{2,1,0:T(8,128)(2,1)S(1)} %bitcast.121, bf16[8,96,384]{2,1,0:T(8,128)(2,1)S(1)} %bitcast.115), custom_call_target="tpu_custom_call" | custom-call | tf_op jit(solution)/shard_map/pallas_call | solution.py:193
  191.2 33.5 %shard_map.149 = (bf16[8,96,768]{2,1,0:T(8,128)(2,1)S(1)}, f32[8,8,128]{2,1,0:T(8,128)S(1)}) custom-call(bf16[8,96,768]{2,1,0:T(8,128)(2,1)S(1)} %bitcast.99, f32[8,8,128]{2,1,0:T(8,128)S(1)} %pad.22.refs_1_), custom_call_target="tpu_custom_call" | custom-call | tf_op jit(solution)/shard_map/pallas_call | solution.py:193
  224.6 3.7 %shard_map.150 = f32[4,8,128]{2,1,0:T(8,128)S(1)} custom-call(f32[8,128]{1,0:T(8,128)S(1)} %reduce_sum.234.refs_0_), custom_call_target="tpu_custom_call" | custom-call | tf_op jit(solution)/shard_map/pallas_call | solution.py:193
  (170 shorter events, 43.7 us)
Async XLA Ops:
  0.6 9.5 %copy-start = (bf16[128,768]{1,0:T(8,128)(2,1)S(1)}, bf16[128,768]{1,0:T(8,128)(2,1)}, u32[]{:S(2)}) copy-start(bf16[128,768]{1,0:T(8,128)(2,1)} %refs_1_.1) | copy-start | bytes 589828
  60.6 2.6 %copy-start.18 = (bf16[512,192]{0,1:T(8,128)(2,1)}, bf16[512,192]{0,1:T(8,128)(2,1)S(1)}, u32[]{:S(2)}) copy-start(bf16[512,192]{0,1:T(8,128)(2,1)S(1)} %slice.229) | copy-start | bytes 589828
  62.6 1.6 copy-start.11
  65.6 10.2 %copy-start.34 = (f32[128]{0:T(128)S(1)}, f32[128]{0:T(128)}, u32[]{:S(2)}) copy-start(f32[128]{0:T(128)} %broadcast_multiply_fusion.8) | copy-start | bytes 1540
  75.9 12.6 %copy-start.33 = (f32[128]{0:T(128)}, f32[128]{0:T(128)S(1)}, u32[]{:S(2)}) copy-start(f32[128]{0:T(128)S(1)} %broadcast_multiply_fusion.11) | copy-start | bytes 1540
  76.8 11.8 %copy-start.36 = (f32[128]{0:T(128)}, f32[128]{0:T(128)S(1)}, u32[]{:S(2)}) copy-start(f32[128]{0:T(128)S(1)} %add_rsqrt_fusion.1) | copy-start | bytes 1540
  90.0 1.2 copy-start.31
  94.9 2.9 %copy-start.25 = (bf16[768,576]{0,1:T(8,128)(2,1)S(1)}, bf16[768,576]{0,1:T(8,128)(2,1)}, u32[]{:S(2)}) copy-start(bf16[768,576]{0,1:T(8,128)(2,1)} %convolution_convert_fusion.1) | copy-start | bytes 2654212
  94.9 3.7 %copy-start.40 = (pred[384]{0:T(512)(128)(4,1)S(1)}, pred[384]{0:T(512)(128)(4,1)}, u32[]{:S(2)}) copy-start(pred[384]{0:T(512)(128)(4,1)} %constant.63.clone.1) | copy-start | bytes 1156
  103.0 3.8 %copy-start.2 = (bf16[768,384]{1,0:T(8,128)(2,1)S(1)}, bf16[768,384]{1,0:T(8,128)(2,1)}, u32[]{:S(2)}) copy-start(bf16[768,384]{1,0:T(8,128)(2,1)} %pad.19.clone) | copy-start | bytes 1769476
  103.0 3.9 %copy-start.5 = (bf16[512,768]{1,0:T(8,128)(2,1)S(1)}, bf16[512,768]{1,0:T(8,128)(2,1)}, u32[]{:S(2)}) copy-start(bf16[512,768]{1,0:T(8,128)(2,1)} %convolution_convert_fusion.3) | copy-start | bytes 2359300
  136.2 9.1 %copy-start.8 = (bf16[128,768]{1,0:T(8,128)(2,1)S(1)}, bf16[128,768]{1,0:T(8,128)(2,1)}, u32[]{:S(2)}) copy-start(bf16[128,768]{1,0:T(8,128)(2,1)} %refs_2_.1) | copy-start | bytes 589828
  147.4 15.1 %copy-start.15 = (bf16[3,64,512]{2,1,0:T(8,128)(2,1)S(1)}, bf16[3,64,512]{2,1,0:T(8,128)(2,1)}, u32[]{:S(2)}) copy-start(bf16[3,64,512]{2,1,0:T(8,128)(2,1)} %copy-done.14) | copy-start | bytes 589828
  161.3 1.9 copy-start.12
  170.5 1.7 copy-start.1
  172.1 16.9 %copy-start.35 = (f32[128]{0:T(128)S(1)}, f32[128]{0:T(128)}, u32[]{:S(2)}) copy-start(f32[128]{0:T(128)} %broadcast_multiply_fusion.8) | copy-start | bytes 1540
  172.2 16.9 %copy-start.37 = (f32[128]{0:T(128)S(1)}, f32[128]{0:T(128)}, u32[]{:S(2)}) copy-start(f32[128]{0:T(128)} %add_rsqrt_fusion) | copy-start | bytes 1540
  188.9 2.2 copy-start.9
  188.9 1.2 copy-start.24
  188.9 2.1 copy-start.32
  189.0 2.1 copy-start.38
  189.0 2.1 copy-start.39
  190.1 38.9 %copy-start.26 = (f32[1,96,288]{2,1,0:T(8,128)S(1)}, f32[1,96,288]{2,1,0:T(8,128)}, u32[]{:S(2)}) copy-start(f32[1,96,288]{2,1,0:T(8,128)} %slice_bitcast_fusion.2) | copy-start | bytes 331780
  191.2 37.7 %copy-start.10 = (bf16[8,96,384]{2,1,0:T(8,128)(2,1)S(1)}, bf16[8,96,384]{2,1,0:T(8,128)(2,1)}, u32[]{:S(2)}) copy-start(bf16[8,96,384]{2,1,0:T(8,128)(2,1)} %copy-done.9) | copy-start | bytes 1769476
  (19 other events, 17.9 us)

commit v2 on v1

--- a/solution.py
+++ b/solution.py
@@ -106,7 +106,7 @@
     count = len(plan)
     sources, targets = refs[:count], refs[count : 2 * count]
     own_sem, send_sem, recv_sem = refs[2 * count :]
-    axes = sorted({axis for _, axis in plan})
+    axes = sorted({axis for _, axis, _ in plan})
     barrier = pltpu.get_barrier_semaphore()
     total = 0
     for axis in axes:
@@ -133,7 +133,7 @@
             device_id_type=pl.DeviceIdType.MESH,
         )
 
-    for which, (kind, axis) in enumerate(plan):
+    for which, (kind, axis, span) in enumerate(plan):
         size = sizes[axis]
         me = lax.axis_index(axis)
         source, target = sources[which], targets[which]
@@ -156,12 +156,12 @@
         else:
             for shift in range(1, size):
                 peer = lax.rem(me + shift, size)
-                piece = source if kind == "gather" else source.at[peer]
+                piece = source if kind == "gather" else source.at[peer, :, span]
                 copy = remote(piece, target.at[me], axis, peer, slot)
                 copy.start()
                 pending.append(copy)
                 slot += 1
-        piece = source if kind != "scatter" else source.at[me]
+        piece = source if kind != "scatter" else source.at[me, :, span]
         copy = pltpu.make_async_copy(piece, target.at[me], own_sem.at[which])
         copy.start()
         local.append(copy)
@@ -181,15 +181,19 @@
 
 
 def exchange(sizes, number, *ops):
-    plan = tuple((kind, axis) for kind, axis, _ in ops)
-    arrays = [array for _, _, array in ops]
+    arrays = [op[2] for op in ops]
+    spans = [slice(*op[3]) if len(op) > 3 else slice(0, op[2].shape[-1]) for op in ops]
+    plan = tuple((op[0], op[1], span) for op, span in zip(ops, spans))
     shapes = [
         jax.ShapeDtypeStruct(
-            array.shape if kind == "scatter" else (sizes[axis],) + array.shape, array.dtype
+            array.shape[:-1] + (span.stop - span.start,)
+            if kind == "scatter"
+            else (sizes[axis],) + array.shape,
+            array.dtype,
         )
-        for kind, axis, array in ops
+        for (kind, axis, span), array in zip(plan, arrays)
     ]
-    slots = sum(slots_of(kind, sizes[axis]) for kind, axis in plan)
+    slots = sum(slots_of(kind, sizes[axis]) for kind, axis, _ in plan)
     return pl.pallas_call(
         functools.partial(exchange_kernel, plan, sizes),
         out_shape=shapes,
@@ -221,6 +225,46 @@
     )
 
 
+def feed_forward_kernel(
+    hidden, rows_ref, up_ref, gate_ref, down_ref, cot_ref, mlp_ref, back_ref, grads_ref
+):
+    bf16 = jnp.bfloat16
+    rows, cot = rows_ref[...], cot_ref[...]
+    inputs = dot_f32(rows, up_ref[...], 1, 0)
+    gate_part = dot_f32(rows, gate_ref[...], 1, 0)
+    activated, gelu_slope = gelu_pair(inputs)
+    hidden_act = (activated * gate_part).astype(bf16)
+    mlp_ref[...] = dot_f32(hidden_act, down_ref[...], 1, 1).astype(bf16)
+    grad_act = dot_f32(cot, down_ref[...], 1, 0)
+    grad_up = (grad_act * gate_part * gelu_slope).astype(bf16)
+    grad_gate = (grad_act * activated).astype(bf16)
+    back_ref[...] = (
+        dot_f32(grad_up, up_ref[...], 1, 1) + dot_f32(grad_gate, gate_ref[...], 1, 1)
+    ).astype(bf16)
+    grads_ref[:, :hidden] = dot_f32(rows, grad_up, 0, 0).astype(bf16)
+    grads_ref[:, hidden : 2 * hidden] = dot_f32(rows, grad_gate, 0, 0).astype(bf16)
+    grads_ref[:, 2 * hidden : 3 * hidden] = dot_f32(cot, hidden_act, 0, 0).astype(bf16)
+    spare = grads_ref.shape[1] - 3 * hidden
+    if spare:
+        grads_ref[:, 3 * hidden :] = jnp.zeros((grads_ref.shape[0], spare), bf16)
+
+
+def feed_forward(hidden, rows, up, gate, down_t, cot):
+    row_count, width = rows.shape
+    padded = -(-3 * hidden // 128) * 128
+    return pl.pallas_call(
+        functools.partial(feed_forward_kernel, hidden),
+        out_shape=[
+            jax.ShapeDtypeStruct((row_count, width), jnp.bfloat16),
+            jax.ShapeDtypeStruct((row_count, width), jnp.bfloat16),
+            jax.ShapeDtypeStruct((width, padded), jnp.bfloat16),
+        ],
+        in_specs=[pl.BlockSpec(memory_space=pltpu.VMEM)] * 5,
+        out_specs=[pl.BlockSpec(memory_space=pltpu.VMEM)] * 3,
+        compiler_params=pltpu.CompilerParams(vmem_limit_bytes=48 << 20),
+    )(rows, up, gate, down_t, cot)
+
+
 def body(sizes, tokens, attn_gain, w_qkv, w_out, mlp_gain, w_in, w_down, cotangent):
     bf16, f32 = jnp.bfloat16, jnp.float32
     groups, members = sizes["dp"], sizes["tensor"]
@@ -239,8 +283,8 @@
         sizes,
         0,
         ("relay", "dp", packed),
-        ("gather", "tensor", tokens),
-        ("gather", "tensor", cotangent),
+        ("relay", "tensor", tokens),
+        ("relay", "tensor", cotangent),
     )
     weights = weights.reshape(width, -1)
     edges = [3 * heads_wide, 4 * heads_wide, 4 * heads_wide + 2 * hidden, 4 * heads_wide + 3 * hidden]
@@ -282,36 +326,28 @@
     hidden_res = residual + total_of(attn_parts)
     normed_two, inv_two = normalize(hidden_res)
     ln_two = (normed_two * mlp_full).astype(bf16)
-    (rows_two,) = exchange(sizes, 2, ("gather", "tensor", ln_two))
+    (rows_two,) = exchange(sizes, 2, ("relay", "tensor", ln_two))
     rows_two = rows_two.reshape(row_count, width)
-    up_gate = dot_f32(rows_two, in_weight, 1, 0)
-    activated, gelu_slope = gelu_pair(up_gate[:, :hidden])
-    gate_part = up_gate[:, hidden:]
-    hidden_act = (activated * gate_part).astype(bf16)
-    mlp_part = dot_f32(hidden_act, down_weight_t, 1, 1).astype(bf16)
-    grad_down_t = dot_f32(grad_rows, hidden_act, 0, 0).astype(bf16)
-    grad_act = dot_f32(grad_rows, down_weight_t, 1, 0)
-    grad_up_gate = jnp.concatenate(
-        [(grad_act * gate_part * gelu_slope).astype(bf16), (grad_act * activated).astype(bf16)], axis=1
-    )
-    grad_in = dot_f32(rows_two, grad_up_gate, 0, 0).astype(bf16)
-    ln_two_part = dot_f32(grad_up_gate, in_weight, 1, 1).astype(bf16)
-    mlp_parts, ln_two_parts, grad_down_parts = exchange(
+    mlp_part, ln_two_part, mlp_grads = feed_forward(
+        hidden, rows_two, in_weight[:, :hidden], in_weight[:, hidden:], down_weight_t, grad_rows
+    )
+    mlp_grads = mlp_grads.reshape(groups, block, -1)
+    mlp_wide = mlp_grads.shape[-1]
+    first = mlp_wide // 384 * 128
+    second = (mlp_wide - first) // 256 * 128 + first
+    ln_two_parts, mlp_grads_a = exchange(
         sizes,
         3,
-        ("scatter", "tensor", mlp_part.reshape(members, own_rows, width)),
         ("scatter", "tensor", ln_two_part.reshape(members, own_rows, width)),
-        ("scatter", "dp", pad_columns(grad_down_t).reshape(groups, block, -1)),
-    )
-    output = (hidden_res + total_of(mlp_parts)).astype(bf16)
+        ("scatter", "dp", mlp_grads, (0, first)),
+    )
     grad_res_two, mlp_gain_part = normalize_back(total_of(ln_two_parts), normed_two, inv_two, mlp_full)
     grad_hidden = cotangent.astype(f32) + grad_res_two
-    half = hidden
-    grad_hidden_rows, grad_in_parts_a = exchange(
+    grad_hidden_rows, mlp_grads_b = exchange(
         sizes,
         4,
-        ("gather", "tensor", grad_hidden.astype(bf16)),
-        ("scatter", "dp", pad_columns(grad_in[:, :half]).reshape(groups, block, -1)),
+        ("relay", "tensor", grad_hidden.astype(bf16)),
+        ("scatter", "dp", mlp_grads, (second, mlp_wide)),
     )
     grad_hidden_rows = grad_hidden_rows.reshape(row_count, width)
     grad_out_t = dot_f32(grad_hidden_rows, mixed_rows, 0, 0).astype(bf16)
@@ -329,29 +365,35 @@
     ).astype(bf16)
     grad_qkv = dot_f32(rows_one, grad_proj, 0, 0).astype(bf16)
     ln_one_part = dot_f32(grad_proj, qkv_weight, 1, 1).astype(bf16)
-    ln_one_parts, grad_in_parts_b = exchange(
+    ln_one_parts, mlp_grads_c, grad_out_parts = exchange(
         sizes,
         5,
         ("scatter", "tensor", ln_one_part.reshape(members, own_rows, width)),
-        ("scatter", "dp", pad_columns(grad_in[:, half:]).reshape(groups, block, -1)),
+        ("scatter", "dp", mlp_grads, (first, second)),
+        ("scatter", "dp", grad_out_t.reshape(groups, block, -1)),
     )
     grad_res_one, attn_gain_part = normalize_back(total_of(ln_one_parts), normed_one, inv_one, attn_full)
     input_grad = grad_hidden + grad_res_one
     gain_parts = jnp.stack([attn_gain_part, mlp_gain_part] + [jnp.zeros_like(attn_gain_part)] * 6)
     gain_parts = pad_columns(jnp.swapaxes(gain_parts.reshape(8, groups, block), 0, 1))
-    late_parts, gain_parts = exchange(
+    late_parts, gain_parts, mlp_parts = exchange(
         sizes,
         6,
-        ("scatter", "dp", jnp.concatenate([grad_qkv, grad_out_t], axis=1).reshape(groups, block, -1)),
+        ("scatter", "dp", grad_qkv.reshape(groups, block, -1)),
         ("scatter", "dp", gain_parts),
-    )
+        ("scatter", "tensor", mlp_part.reshape(members, own_rows, width)),
+    )
+    output = (hidden_res + total_of(mlp_parts)).astype(bf16)
     (gain_groups,) = exchange(sizes, 7, ("gather", "tensor", total_of(gain_parts)))
     gain_sum = total_of(gain_groups)
     late = total_of(late_parts)
     grad_w_qkv = jnp.stack([late[:, i * heads_wide : (i + 1) * heads_wide] for i in range(3)])
-    grad_w_out = late[:, 3 * heads_wide : 4 * heads_wide].T
-    grad_w_in = jnp.stack([total_of(grad_in_parts_a)[:, :hidden], total_of(grad_in_parts_b)[:, :hidden]])
-    grad_w_down = total_of(grad_down_parts)[:, :hidden].T
+    grad_w_out = total_of(grad_out_parts).T
+    mlp_sums = jnp.concatenate(
+        [total_of(mlp_grads_a), total_of(mlp_grads_c), total_of(mlp_grads_b)], axis=1
+    )
+    grad_w_in = jnp.stack([mlp_sums[:, :hidden], mlp_sums[:, hidden : 2 * hidden]])
+    grad_w_down = mlp_sums[:, 2 * hidden : 3 * hidden].T
     return (
         output,
         input_grad,

time: 233 us -> 199 us (0.85)
  local copies, waits for them, and re-layouts: 32.3 us -> 15.5 us
  other arithmetic: 22.3 us -> 15 us
  Pallas kernels: 159 us -> 154 us
  matrix products: 16.3 us -> 12.7 us
    unnamed x93 -> x70, local copies, waits for them, and re-layouts: 17.2 us -> 5.88 us
    pallas_call x8, Pallas kernels: 159 us -> 149 us  [exchange(): pl.pallas_call(functools.partial(exchange_kernel, plan, sizes), out_shape...]
    dot_general x12 -> x6, matrix products: 12.5 us -> 6.83 us  [dot_f32(): lax.dot_general(left, right, (((left_dim,), (right_dim,)), ((), ())), pre...]
    pallas_call x0 -> x1, Pallas kernels: none -> 5.4 us  [feed_forward(): pl.pallas_call(functools.partial(feed_forward_kernel, hidden), out_shape=...]
    pad x5 -> x2, local copies, waits for them, and re-layouts: 4.39 us -> 0.65 us  [pad_columns(): return jnp.pad(array, [(0, 0)] * (array.ndim - 1) + [(0, extra)])]
where the time goes in v2:
time: 199 us
  Pallas kernels  154 us (77%)
  local copies, waits for them, and re-layouts  15.5 us (8%)
  other arithmetic  15 us (8%)
  matrix products  12.7 us (6%)
    pallas_call x8, Pallas kernels, exchange(): pl.pallas_call(functools.partial(exchange_kernel, plan, sizes), out_shape...  149 us
    dot_general x6, matrix products, dot_f32(): lax.dot_general(left, right, (((left_dim,), (right_dim,)), ((), ())), pre...  6.83 us
    unnamed x70, local copies, waits for them, and re-layouts  5.88 us
    pallas_call x1, Pallas kernels, feed_forward(): pl.pallas_call(functools.partial(feed_forward_kernel, hidden), out_shape=...  5.4 us

profile of v2, /device:TPU:0, one launch (start us, length us, event | category | flops | bytes accessed | tf_op | source)
XLA Modules:
  0.0 198.6 jit_solution(13133197026744105760)
XLA Ops:
  0.7 1.1 convert_reduce_fusion.10
  4.7 0.9 copy.40
  5.6 1.0 copy.41
  7.5 0.9 slice_bitcast_fusion.4
  8.7 1.0 broadcast_multiply_fusion.3
  9.7 43.0 %shard_map.143 = (bf16[8,96,1664]{2,1,0:T(8,128)(2,1)S(1)}, bf16[4,128,768]{2,1,0:T(8,128)(2,1)S(1)}, bf16[4,128,768]{2,1,0:T(8,128)(2,1)S(1)}) custom-call(bf16[96,1664]{1,0:T(8,128)(2,1)S(1)} %pad.8.refs_0_, bf16[128,768]{1,0:T(8,128)(2,1)S(1)} %copy-done.3, bf16[128,768]{1,0:T(8,128)(2,1)S(1)} %copy-done.4), custom_call_target="tpu_custom_call" | custom-call | tf_op jit(solution)/shard_map/pallas_call | solution.py:197
  58.3 10.0 %shard_map.144 = bf16[4,128,768]{2,1,0:T(8,128)(2,1)S(1)} custom-call(bf16[4,128,768]{2,1,0:T(8,128)(2,1)S(1)} %bitcast.104), custom_call_target="tpu_custom_call" | custom-call | tf_op jit(solution)/shard_map/pallas_call | solution.py:197
  69.6 9.4 %shard_map.145 = bf16[4,128,768]{2,1,0:T(8,128)(2,1)S(1)} custom-call(bf16[128,768]{1,0:T(8,128)(2,1)S(1)} %multiply_convert_fusion.1.refs_0_), custom_call_target="tpu_custom_call" | custom-call | tf_op jit(solution)/shard_map/pallas_call | solution.py:197
  79.0 5.4 %shard_map.146 = (bf16[512,768]{1,0:T(8,128)(2,1)S(1)}, bf16[512,768]{1,0:T(8,128)(2,1)S(1)}, bf16[768,896]{1,0:T(8,128)(2,1)}) custom-call(bf16[512,768]{1,0:T(8,128)(2,1)S(1)} %bitcast.105, bf16[768,288]{1,0:T(8,128)(2,1)S(1)} %get-tuple-element.78.up_ref, bf16[768,288]{1,0:T(8,128)(2,1)S(1)} %get-tuple-element.77.gate_ref, ...), custom_call_target="tpu_custom_call" | custom-call | tf_op jit(solution)/shard_map/pallas_call | solution.py:255
  84.4 1.3 copy-done
  85.7 18.1 %shard_map.147 = (bf16[4,128,768]{2,1,0:T(8,128)(2,1)S(1)}, bf16[8,96,256]{2,1,0:T(8,128)(2,1)S(1)}) custom-call(bf16[4,128,768]{2,1,0:T(8,128)(2,1)S(1)} %bitcast.108, bf16[8,96,896]{2,1,0:T(8,128)(2,1)S(1)} %bitcast.92), custom_call_target="tpu_custom_call" | custom-call | tf_op jit(solution)/shard_map/pallas_call | solution.py:197
  104.7 1.2 multiply_reduce_fusion.2
  107.3 1.9 fusion.41
  109.2 15.0 %shard_map.148 = (bf16[4,128,768]{2,1,0:T(8,128)(2,1)S(1)}, bf16[8,96,384]{2,1,0:T(8,128)(2,1)S(1)}) custom-call(bf16[128,768]{1,0:T(8,128)(2,1)S(1)} %get-tuple-element.72.refs_0_, bf16[8,96,896]{2,1,0:T(8,128)(2,1)S(1)} %bitcast.93), custom_call_target="tpu_custom_call" | custom-call | tf_op jit(solution)/shard_map/pallas_call | solution.py:197
  125.0 1.6 convolution_convert_fusion.5
  127.2 2.7 %convolution_convert_fusion.4 = bf16[3,64,512]{2,1,0:T(8,128)(2,1)S(1)} fusion(bf16[512,3,64]{0,2,1:T(8,128)(2,1)S(1)} %bitcast.116, f32[3,512,512]{1,2,0:T(8,128)} %copy-done.6, f32[3,512]{1,0:T(4,128)S(1)} %log_add_fusion), kind=kOutput, calls=%fused_computation.22 | convolution fusion | flops 103120896 | bytes 3545088 | tf_op jit(solution)/shard_map/hqk,qhd->khd/dot_general | solution.py:91
  130.0 0.9 multiply_convert_fusion
  133.1 2.1 %convolution_convert_fusion.1 = bf16[512,768]{1,0:T(8,128)(2,1)S(1)} fusion(bf16[768,1664]{1,0:T(8,128)(2,1)} %bitcast.100, bf16[512,192]{0,1:T(8,128)(2,1)S(1)} %bitcast.124, bf16[512,192]{0,1:T(8,128)(2,1)S(1)} %bitcast.128, bf16[512,192]{0,1:T(8,128)(2,1)S(1)} %bitcast.126), kind=kOutput, calls=%fused_computation.16 | convolution fusion | flops 455147520 | bytes 2359296 | tf_op jit(solution)/shard_map/dot_general | solution.py:223
  135.2 1.6 convolution_convert_fusion
  136.7 22.5 %shard_map.149 = (bf16[4,128,768]{2,1,0:T(8,128)(2,1)S(1)}, bf16[8,96,256]{2,1,0:T(8,128)(2,1)S(1)}, bf16[8,96,192]{2,1,0:T(8,128)(2,1)S(1)}) custom-call(bf16[4,128,768]{2,1,0:T(8,128)(2,1)S(1)} %bitcast.110, bf16[8,96,896]{2,1,0:T(8,128)(2,1)S(1)} %bitcast.94, bf16[8,96,192]{2,1,0:T(8,128)(2,1)S(1)} %bitcast.106), custom_call_target="tpu_custom_call" | custom-call | tf_op jit(solution)/shard_map/pallas_call | solution.py:197
  159.7 0.9 fusion.16
  162.3 1.5 copy.49
  163.9 27.0 %shard_map.150 = (bf16[8,96,576]{2,1,0:T(8,128)(2,1)S(1)}, f32[8,8,128]{2,1,0:T(8,128)S(1)}, bf16[4,128,768]{2,1,0:T(8,128)(2,1)S(1)}) custom-call(bf16[8,96,576]{2,1,0:T(8,128)(2,1)S(1)} %bitcast.101, f32[8,8,128]{2,1,0:T(8,128)S(1)} %copy-done.5, bf16[4,128,768]{2,1,0:T(8,128)(2,1)S(1)} %bitcast.107), custom_call_target="tpu_custom_call" | custom-call | tf_op jit(solution)/shard_map/pallas_call | solution.py:197
  191.7 3.7 %shard_map.151 = f32[4,8,128]{2,1,0:T(8,128)S(1)} custom-call(f32[8,128]{1,0:T(8,128)S(1)} %reduce_sum.243.refs_0_), custom_call_target="tpu_custom_call" | custom-call | tf_op jit(solution)/shard_map/pallas_call | solution.py:197
  (138 shorter events, 22.5 us)
Async XLA Ops:
  0.6 9.0 %copy-start.3 = (bf16[128,768]{1,0:T(8,128)(2,1)S(1)}, bf16[128,768]{1,0:T(8,128)(2,1)}, u32[]{:S(2)}) copy-start(bf16[128,768]{1,0:T(8,128)(2,1)} %refs_1_.1) | copy-start | bytes 589828
  0.6 9.0 %copy-start.4 = (bf16[128,768]{1,0:T(8,128)(2,1)S(1)}, bf16[128,768]{1,0:T(8,128)(2,1)}, u32[]{:S(2)}) copy-start(bf16[128,768]{1,0:T(8,128)(2,1)} %refs_2_.1) | copy-start | bytes 589828
  1.8 66.6 %copy-start.27 = (f32[128]{0:T(128)}, f32[128]{0:T(128)S(1)}, u32[]{:S(2)}) copy-start(f32[128]{0:T(128)S(1)} %broadcast_multiply_fusion.8) | copy-start | bytes 1540
  52.7 5.0 %copy-start.2 = (bf16[8,96,1664]{2,1,0:T(8,128)(2,1)}, bf16[8,96,1664]{2,1,0:T(8,128)(2,1)S(1)}, u32[]{:S(2)}) copy-start(bf16[8,96,1664]{2,1,0:T(8,128)(2,1)S(1)} %get-tuple-element.25) | copy-start | bytes 7667716
  54.8 2.2 %copy-start.14 = (bf16[512,192]{0,1:T(8,128)(2,1)}, bf16[512,192]{0,1:T(8,128)(2,1)S(1)}, u32[]{:S(2)}) copy-start(bf16[512,192]{0,1:T(8,128)(2,1)S(1)} %slice.184) | copy-start | bytes 589828
  56.5 12.1 %copy-start.6 = (f32[3,512,512]{1,2,0:T(8,128)}, f32[3,512,512]{1,2,0:T(8,128)S(1)}, u32[]{:S(2)}) copy-start(f32[3,512,512]{1,2,0:T(8,128)S(1)} %get-tuple-element.116) | copy-start | bytes 9437188
  57.7 10.7 %copy-start.10 = (bf16[3,64,512]{2,1,0:T(8,128)(2,1)}, bf16[3,64,512]{2,1,0:T(8,128)(2,1)S(1)}, u32[]{:S(2)}) copy-start(bf16[3,64,512]{2,1,0:T(8,128)(2,1)S(1)} %convolution_convert_fusion.6) | copy-start | bytes 589828
  68.6 38.6 %copy-start.8 = (f32[128,768]{1,0:T(8,128)}, f32[128,768]{1,0:T(8,128)S(1)}, u32[]{:S(2)}) copy-start(f32[128,768]{1,0:T(8,128)S(1)} %get-tuple-element.75) | copy-start | bytes 1179652
  68.6 36.0 %copy-start.26 = (f32[128]{0:T(128)}, f32[128]{0:T(128)S(1)}, u32[]{:S(2)}) copy-start(f32[128]{0:T(128)S(1)} %broadcast_multiply_fusion.11) | copy-start | bytes 1540
  69.5 35.2 %copy-start.29 = (f32[128]{0:T(128)}, f32[128]{0:T(128)S(1)}, u32[]{:S(2)}) copy-start(f32[128]{0:T(128)S(1)} %add_rsqrt_fusion.1) | copy-start | bytes 1540
  103.8 5.4 %copy-start.1 = (bf16[768,896]{1,0:T(8,128)(2,1)S(1)}, bf16[768,896]{1,0:T(8,128)(2,1)}, u32[]{:S(2)}) copy-start(bf16[768,896]{1,0:T(8,128)(2,1)} %get-tuple-element.28) | copy-start | bytes 4128772
  109.2 17.4 %copy-start.11 = (bf16[3,64,512]{2,1,0:T(8,128)(2,1)S(1)}, bf16[3,64,512]{2,1,0:T(8,128)(2,1)}, u32[]{:S(2)}) copy-start(bf16[3,64,512]{2,1,0:T(8,128)(2,1)} %copy-done.10) | copy-start | bytes 589828
  127.0 2.9 %copy-start.15 = (bf16[512,192]{0,1:T(8,128)(2,1)S(1)}, bf16[512,192]{0,1:T(8,128)(2,1)}, u32[]{:S(2)}) copy-start(bf16[512,192]{0,1:T(8,128)(2,1)} %copy-done.14) | copy-start | bytes 589828
  127.2 2.9 %copy-start.7 = (f32[3,512,512]{1,2,0:T(8,128)S(1)}, f32[3,512,512]{1,2,0:T(8,128)}, u32[]{:S(2)}) copy-start(f32[3,512,512]{1,2,0:T(8,128)} %copy-done.6) | copy-start | bytes 9437188
  133.1 2.1 %copy-start.13 = (bf16[512,768]{1,0:T(8,128)(2,1)S(1)}, bf16[512,768]{1,0:T(8,128)(2,1)}, u32[]{:S(2)}) copy-start(bf16[512,768]{1,0:T(8,128)(2,1)} %copy-done.12) | copy-start | bytes 2359300
  136.7 22.7 %copy-start.28 = (f32[128]{0:T(128)S(1)}, f32[128]{0:T(128)}, u32[]{:S(2)}) copy-start(f32[128]{0:T(128)} %copy-done.27) | copy-start | bytes 1540
  136.7 22.7 %copy-start.30 = (f32[128]{0:T(128)S(1)}, f32[128]{0:T(128)}, u32[]{:S(2)}) copy-start(f32[128]{0:T(128)} %add_rsqrt_fusion) | copy-start | bytes 1540
  136.7 22.9 %copy-start.20 = (f32[128,768]{1,0:T(8,128)S(1)}, f32[128,768]{1,0:T(8,128)}, u32[]{:S(2)}) copy-start(f32[128,768]{1,0:T(8,128)} %get-tuple-element.73) | copy-start | bytes 1179652
  159.2 1.4 copy-start.25
  159.3 1.4 copy-start.31
  161.5 2.4 %copy-start.5 = (f32[8,8,128]{2,1,0:T(8,128)S(1)}, f32[8,8,128]{2,1,0:T(8,128)}, u32[]{:S(2)}) copy-start(f32[8,8,128]{2,1,0:T(8,128)} %pad.9.refs_1_) | copy-start | bytes 98308
  163.8 27.1 %copy-start.9 = (f32[128,768]{1,0:T(8,128)S(1)}, f32[128,768]{1,0:T(8,128)}, u32[]{:S(2)}) copy-start(f32[128,768]{1,0:T(8,128)} %copy-done.8) | copy-start | bytes 1179652
  163.9 32.1 %copy-start.21 = (f32[96,384]{1,0:T(8,128)S(1)}, f32[96,384]{1,0:T(8,128)}, u32[]{:S(2)}) copy-start(f32[96,384]{1,0:T(8,128)} %convert_reduce_fusion.5) | copy-start | bytes 442372
  163.9 32.1 %copy-start.24 = (f32[96,256]{1,0:T(8,128)S(1)}, f32[96,256]{1,0:T(8,128)}, u32[]{:S(2)}) copy-start(f32[96,256]{1,0:T(8,128)} %convert_reduce_fusion.8) | copy-start | bytes 294916
  (9 other events, 9.8 us)

commit v3 on v2

--- a/solution.py
+++ b/solution.py
@@ -137,11 +137,28 @@
         size = sizes[axis]
         me = lax.axis_index(axis)
         source, target = sources[which], targets[which]
+        outer = size // 2
+        column = lax.rem(me, 2)
+        row = me // 2
+        partner = row * 2 + 1 - column
+        if kind == "half":
+            copy = remote(source.at[:, 1 - column, :, span], target, axis, partner, slot)
+            copy.start()
+            pending.append(copy)
+            slot += 1
+            continue
+        if kind == "outer":
+            for shift in range(1, outer):
+                other = lax.rem(row + shift, outer)
+                copy = remote(source.at[other], target.at[row], axis, other * 2 + column, slot)
+                copy.start()
+                pending.append(copy)
+                slot += 1
+            copy = pltpu.make_async_copy(source.at[row], target.at[row], own_sem.at[which])
+            copy.start()
+            local.append(copy)
+            continue
         if kind == "relay":
-            outer = size // 2
-            column = lax.rem(me, 2)
-            row = me // 2
-            partner = row * 2 + 1 - column
             for shift in range(1, outer):
                 peer = lax.rem(row + shift, outer) * 2 + column
                 copy = remote(source, target.at[me], axis, peer, slot)
@@ -177,7 +194,14 @@
 
 
 def slots_of(kind, size):
-    return 2 * (size // 2 - 1) + 1 if kind == "relay" else size - 1
+    outer = size // 2
+    return {"relay": 2 * outer - 1, "half": 1, "outer": outer - 1}.get(kind, size - 1)
+
+
+def shape_of(kind, size, shape, wide):
+    if kind == "half":
+        return (shape[0], shape[2], wide)
+    return {"scatter": shape[:-1] + (wide,), "outer": shape}.get(kind, (size,) + shape)
 
 
 def exchange(sizes, number, *ops):
@@ -186,10 +210,7 @@
     plan = tuple((op[0], op[1], span) for op, span in zip(ops, spans))
     shapes = [
         jax.ShapeDtypeStruct(
-            array.shape[:-1] + (span.stop - span.start,)
-            if kind == "scatter"
-            else (sizes[axis],) + array.shape,
-            array.dtype,
+            shape_of(kind, sizes[axis], array.shape, span.stop - span.start), array.dtype
         )
         for (kind, axis, span), array in zip(plan, arrays)
     ]
@@ -272,28 +293,31 @@
     width = block * groups
     heads_wide, hidden = w_qkv.shape[2], w_in.shape[2]
     own_rows = tokens.shape[0]
-    packed = pad_columns(
-        jnp.concatenate(
-            [w_qkv[0], w_qkv[1], w_qkv[2], w_out.T, w_in[0], w_in[1], w_down.T]
-            + [attn_gain[:, None], mlp_gain[:, None]],
-            axis=1,
-        )
-    )
-    weights, token_rows, grad_rows = exchange(
+    packed = jnp.concatenate([w_qkv[0], w_qkv[1], w_qkv[2], w_out.T], axis=1)
+    gain_tile = jnp.pad(jnp.stack([attn_gain, mlp_gain]), [(0, 14), (0, -block % 128)])
+    weights, gain_tiles, token_rows, grad_rows = exchange(
         sizes,
         0,
         ("relay", "dp", packed),
+        ("relay", "dp", gain_tile),
         ("relay", "tensor", tokens),
         ("relay", "tensor", cotangent),
     )
     weights = weights.reshape(width, -1)
-    edges = [3 * heads_wide, 4 * heads_wide, 4 * heads_wide + 2 * hidden, 4 * heads_wide + 3 * hidden]
-    qkv_weight = weights[:, : edges[0]]
-    out_weight_t = weights[:, edges[0] : edges[1]]
-    in_weight = weights[:, edges[1] : edges[2]]
-    down_weight_t = weights[:, edges[2] : edges[3]]
-    gains = weights[:, edges[3] : edges[3] + 2].astype(f32).T
-    attn_full, mlp_full = gains[0:1], gains[1:2]
+    qkv_weight = weights[:, : 3 * heads_wide]
+    out_weight_t = weights[:, 3 * heads_wide :]
+    attn_full = gain_tiles[:, 0, :block].reshape(1, width).astype(f32)
+    mlp_full = gain_tiles[:, 1, :block].reshape(1, width).astype(f32)
+    outer = groups // 2
+    column = lax.rem(lax.axis_index("dp"), 2)
+
+    def quarter(array):
+        return array.reshape(outer, 2, block, -1)
+
+    def half_sum(array, received, low, high):
+        own = lax.dynamic_index_in_dim(quarter(array)[..., low:high], column, 1, keepdims=False)
+        return (own.astype(f32) + received.astype(f32)).astype(bf16)
+
     row_count = own_rows * members
     grad_rows = grad_rows.reshape(row_count, width)
     residual = tokens.astype(f32)
@@ -320,34 +344,42 @@
     attn_mix, log_total = over_sequences(attend, (queries, key_rows, value_rows))
     mixed_rows = attn_mix.reshape(flat_shape)
     attn_part = dot_f32(mixed_rows, out_weight_t, 1, 1).astype(bf16)
-    (attn_parts,) = exchange(
-        sizes, 1, ("scatter", "tensor", attn_part.reshape(members, own_rows, width))
-    )
+    attn_parts, up_weight, down_weight_t = exchange(
+        sizes,
+        1,
+        ("scatter", "tensor", attn_part.reshape(members, own_rows, width)),
+        ("relay", "dp", w_in[0]),
+        ("relay", "dp", w_down.T),
+    )
+    up_weight = up_weight.reshape(width, -1)
+    down_weight_t = down_weight_t.reshape(width, -1)
     hidden_res = residual + total_of(attn_parts)
     normed_two, inv_two = normalize(hidden_res)
     ln_two = (normed_two * mlp_full).astype(bf16)
-    (rows_two,) = exchange(sizes, 2, ("relay", "tensor", ln_two))
+    rows_two, gate_weight = exchange(
+        sizes, 2, ("relay", "tensor", ln_two), ("relay", "dp", w_in[1])
+    )
+    gate_weight = gate_weight.reshape(width, -1)
     rows_two = rows_two.reshape(row_count, width)
     mlp_part, ln_two_part, mlp_grads = feed_forward(
-        hidden, rows_two, in_weight[:, :hidden], in_weight[:, hidden:], down_weight_t, grad_rows
-    )
-    mlp_grads = mlp_grads.reshape(groups, block, -1)
+        hidden, rows_two, up_weight, gate_weight, down_weight_t, grad_rows
+    )
     mlp_wide = mlp_grads.shape[-1]
-    first = mlp_wide // 384 * 128
-    second = (mlp_wide - first) // 256 * 128 + first
+    first = mlp_wide // 256 * 128
     ln_two_parts, mlp_grads_a = exchange(
         sizes,
         3,
         ("scatter", "tensor", ln_two_part.reshape(members, own_rows, width)),
-        ("scatter", "dp", mlp_grads, (0, first)),
+        ("half", "dp", quarter(mlp_grads), (0, first)),
     )
     grad_res_two, mlp_gain_part = normalize_back(total_of(ln_two_parts), normed_two, inv_two, mlp_full)
     grad_hidden = cotangent.astype(f32) + grad_res_two
-    grad_hidden_rows, mlp_grads_b = exchange(
+    grad_hidden_rows, mlp_grads_b, mlp_sums_a = exchange(
         sizes,
         4,
         ("relay", "tensor", grad_hidden.astype(bf16)),
-        ("scatter", "dp", mlp_grads, (second, mlp_wide)),
+        ("half", "dp", quarter(mlp_grads), (first, mlp_wide)),
+        ("outer", "dp", half_sum(mlp_grads, mlp_grads_a, 0, first)),
     )
     grad_hidden_rows = grad_hidden_rows.reshape(row_count, width)
     grad_out_t = dot_f32(grad_hidden_rows, mixed_rows, 0, 0).astype(bf16)
@@ -365,32 +397,38 @@
     ).astype(bf16)
     grad_qkv = dot_f32(rows_one, grad_proj, 0, 0).astype(bf16)
     ln_one_part = dot_f32(grad_proj, qkv_weight, 1, 1).astype(bf16)
-    ln_one_parts, mlp_grads_c, grad_out_parts = exchange(
+    ln_one_parts, mlp_sums_b, grad_out_half = exchange(
         sizes,
         5,
         ("scatter", "tensor", ln_one_part.reshape(members, own_rows, width)),
-        ("scatter", "dp", mlp_grads, (first, second)),
-        ("scatter", "dp", grad_out_t.reshape(groups, block, -1)),
+        ("outer", "dp", half_sum(mlp_grads, mlp_grads_b, first, mlp_wide)),
+        ("half", "dp", quarter(grad_out_t)),
     )
     grad_res_one, attn_gain_part = normalize_back(total_of(ln_one_parts), normed_one, inv_one, attn_full)
     input_grad = grad_hidden + grad_res_one
     gain_parts = jnp.stack([attn_gain_part, mlp_gain_part] + [jnp.zeros_like(attn_gain_part)] * 6)
     gain_parts = pad_columns(jnp.swapaxes(gain_parts.reshape(8, groups, block), 0, 1))
-    late_parts, gain_parts, mlp_parts = exchange(
+    qkv_half, gain_parts, mlp_parts, grad_out_parts = exchange(
         sizes,
         6,
-        ("scatter", "dp", grad_qkv.reshape(groups, block, -1)),
+        ("half", "dp", quarter(grad_qkv)),
         ("scatter", "dp", gain_parts),
         ("scatter", "tensor", mlp_part.reshape(members, own_rows, width)),
+        ("outer", "dp", half_sum(grad_out_t, grad_out_half, 0, heads_wide)),
     )
     output = (hidden_res + total_of(mlp_parts)).astype(bf16)
-    (gain_groups,) = exchange(sizes, 7, ("gather", "tensor", total_of(gain_parts)))
+    gain_groups, late_parts = exchange(
+        sizes,
+        7,
+        ("gather", "tensor", total_of(gain_parts)),
+        ("outer", "dp", half_sum(grad_qkv, qkv_half, 0, 3 * heads_wide)),
+    )
     gain_sum = total_of(gain_groups)
     late = total_of(late_parts)
     grad_w_qkv = jnp.stack([late[:, i * heads_wide : (i + 1) * heads_wide] for i in range(3)])
     grad_w_out = total_of(grad_out_parts).T
     mlp_sums = jnp.concatenate(
-        [total_of(mlp_grads_a), total_of(mlp_grads_c), total_of(mlp_grads_b)], axis=1
+        [total_of(mlp_sums_a), total_of(mlp_sums_b)], axis=1
     )
     grad_w_in = jnp.stack([mlp_sums[:, :hidden], mlp_sums[:, hidden : 2 * hidden]])
     grad_w_down = mlp_sums[:, 2 * hidden : 3 * hidden].T

time: 199 us -> 187 us (0.940)
  Pallas kernels: 154 us -> 132 us
  local copies, waits for them, and re-layouts: 15.5 us -> 25 us
  matrix products: 12.7 us -> 8.99 us
  other arithmetic: 15 us -> 18.3 us
    pallas_call x8, Pallas kernels: 149 us -> 127 us  [exchange(): pl.pallas_call(functools.partial(exchange_kernel, plan, sizes), out_shape...]
    unnamed x70 -> x105, local copies, waits for them, and re-layouts: 5.88 us -> 16.2 us
    reshape x0 -> x2, local copies, waits for them, and re-layouts: none -> 4.06 us  [quarter(): return array.reshape(outer, 2, block, -1)]
    dot_general x1, matrix products: 2.7 us -> 0.66 us  [attend_back(): jnp.einsum('hqk,qhd->khd', prob_rounded, grad_mix, preferred_element_type...]
where the time goes in v3:
time: 187 us; the launch traced here: 186 us
  Pallas kernels  132 us (71%)
  local copies, waits for them, and re-layouts  25 us (13%)
  other arithmetic  18.3 us (10%)
  matrix products  8.99 us (5%)
    pallas_call x8, Pallas kernels, exchange(): pl.pallas_call(functools.partial(exchange_kernel, plan, sizes), out_shape...  127 us
    unnamed x105, local copies, waits for them, and re-layouts  16.2 us
    pallas_call x1, Pallas kernels, feed_forward(): pl.pallas_call(functools.partial(feed_forward_kernel, hidden), out_shape=...  5.4 us
    dot_general x6, matrix products, dot_f32(): lax.dot_general(left, right, (((left_dim,), (right_dim,)), ((), ())), pre...  5.19 us
    reshape x2, local copies, waits for them, and re-layouts, quarter(): return array.reshape(outer, 2, block, -1)  4.06 us

profile of v3, /device:TPU:0, one launch (start us, length us, event | category | flops | bytes accessed | tf_op | source)
XLA Modules:
  0.0 185.8 jit_solution(6105331829189400006)
XLA Ops:
  5.0 24.9 %shard_map.143 = (bf16[8,96,768]{2,1,0:T(8,128)(2,1)S(1)}, bf16[8,16,128]{2,1,0:T(8,128)(2,1)S(1)}, bf16[4,128,768]{2,1,0:T(8,128)(2,1)S(1)}, bf16[4,128,768]{2,1,0:T(8,128)(2,1)S(1)}) custom-call(bf16[96,768]{1,0:T(8,128)(2,1)S(1)} %pad_maximum_fusion.6.refs_0_, bf16[16,128]{1,0:T(8,128)(2,1)S(1)} %fusion.40.refs_1_, bf16[128,768]{1,0:T(8,128)(2,1)S(1)} %copy-done.2, ...), custom_call_target="tpu_custom_call" | custom-call | tf_op jit(solution)/shard_map/pallas_call | solution.py:218
  35.4 1.1 copy-done.19
  38.5 21.6 %shard_map.144 = (bf16[4,128,768]{2,1,0:T(8,128)(2,1)S(1)}, bf16[8,96,288]{2,1,0:T(8,128)(2,1)S(1)}, bf16[8,96,288]{2,1,0:T(8,128)(2,1)S(1)}) custom-call(bf16[4,128,768]{2,1,0:T(8,128)(2,1)S(1)} %bitcast.120, bf16[96,288]{1,0:T(8,128)(2,1)S(1)} %get-tuple-element.116.refs_1_, bf16[96,288]{1,0:T(8,128)(2,1)S(1)} %bitcast.133), custom_call_target="tpu_custom_call" | custom-call | tf_op jit(solution)/shard_map/pallas_call | solution.py:218
  60.3 1.3 fusion.51
  61.7 1.2 multiply_reduce_fusion.5
  63.0 1.1 multiply_convert_fusion.1.refs_0_
  64.1 15.6 %shard_map.145 = (bf16[4,128,768]{2,1,0:T(8,128)(2,1)S(1)}, bf16[8,96,288]{2,1,0:T(8,128)(2,1)S(1)}) custom-call(bf16[128,768]{1,0:T(8,128)(2,1)S(1)} %multiply_convert_fusion.1.refs_0_, bf16[96,288]{1,0:T(8,128)(2,1)S(1)} %copy-done.18), custom_call_target="tpu_custom_call" | custom-call | tf_op jit(solution)/shard_map/pallas_call | solution.py:218
  79.8 1.1 copy-done.13
  80.8 5.4 %shard_map.146 = (bf16[512,768]{1,0:T(8,128)(2,1)S(1)}, bf16[512,768]{1,0:T(8,128)(2,1)S(1)}, bf16[768,896]{1,0:T(8,128)(2,1)}) custom-call(bf16[512,768]{1,0:T(8,128)(2,1)S(1)} %bitcast.129, bf16[768,288]{1,0:T(8,128)(2,1)S(1)} %bitcast.130, bf16[768,288]{1,0:T(8,128)(2,1)S(1)} %bitcast.132, bf16[768,288]{1,0:T(8,128)(2,1)S(1)} %bitcast.131, ...), custom_call_target="tpu_custom_call" | custom-call | tf_op jit(solution)/shard_map/pallas_call | solution.py:276
  86.2 1.6 copy-done
  87.8 10.5 %shard_map.147 = (bf16[4,128,768]{2,1,0:T(8,128)(2,1)S(1)}, bf16[4,96,384]{2,1,0:T(8,128)(2,1)S(1)}) custom-call(bf16[4,128,768]{2,1,0:T(8,128)(2,1)S(1)} %bitcast.125, bf16[4,2,96,896]{3,2,1,0:T(8,128)(2,1)S(1)} %bitcast.112), custom_call_target="tpu_custom_call" | custom-call | tf_op jit(solution)/shard_map/pallas_call | solution.py:218
  99.4 1.4 convert_reduce_fusion.2
  100.7 1.8 multiply_reduce_fusion.2
  102.6 2.0 %fusion.50 = (bf16[128,768]{1,0:T(8,128)(2,1)S(1)}, f32[128,768]{1,0:T(8,128)}) fusion(f32[128]{0:T(128)S(1)} %broadcast_multiply_fusion.9, f32[128,768]{1,0:T(8,128)} %get-tuple-element.95, f32[128]{0:T(128)} %copy-done.45, f32[128]{0:T(128)S(1)} %broadcast_multiply_fusion.10, f32[128,768]{1,0:T(8,128)S(1)} %convert_reduce_fusion.2, f32[768]{0:T(1024)S(1)} %reshape.283, ...), kind=kLoop, calls=%fused_computation.141 | loop fusion | flops 983040 | bytes 1577984 | tf_op jit(solution)/shard_map/convert_element_type | solution.py:380
  104.6 14.5 %shard_map.148 = (bf16[4,128,768]{2,1,0:T(8,128)(2,1)S(1)}, bf16[4,96,512]{2,1,0:T(8,128)(2,1)S(1)}, bf16[4,96,384]{2,1,0:T(8,128)(2,1)S(1)}) custom-call(bf16[128,768]{1,0:T(8,128)(2,1)S(1)} %get-tuple-element.92.refs_0_, bf16[4,2,96,896]{3,2,1,0:T(8,128)(2,1)S(1)} %bitcast.114, bf16[4,96,384]{2,1,0:T(8,128)(2,1)S(1)} %fusion.9.refs_2_), custom_call_target="tpu_custom_call" | custom-call | tf_op jit(solution)/shard_map/pallas_call | solution.py:218
  121.6 2.2 %reshape.279 = bf16[4,2,96,192]{2,1,0,3:T(2,128)(2,1)} reshape(bf16[768,192]{0,1:T(8,128)(2,1)} %convolution_convert_fusion.3) | data formatting | bytes 589824 | tf_op jit(solution)/shard_map/reshape | solution.py:315
  123.8 1.9 %copy.52.refs_2_ = bf16[4,2,96,192]{3,2,1,0:T(8,128)(2,1)} copy(bf16[4,2,96,192]{2,1,0,3:T(2,128)(2,1)} %reshape.279) | data formatting | bytes 589824 | tf_op jit(solution)/shard_map/reshape | solution.py:315
  133.2 11.2 %shard_map.149 = (bf16[4,128,768]{2,1,0:T(8,128)(2,1)S(1)}, bf16[4,96,512]{2,1,0:T(8,128)(2,1)S(1)}, bf16[4,96,192]{2,1,0:T(8,128)(2,1)S(1)}) custom-call(bf16[4,128,768]{2,1,0:T(8,128)(2,1)S(1)} %bitcast.126, bf16[4,96,512]{2,1,0:T(8,128)(2,1)S(1)} %fusion.8.refs_1_, bf16[4,2,96,192]{3,2,1,0:T(8,128)(2,1)S(1)} %copy-done.4), custom_call_target="tpu_custom_call" | custom-call | tf_op jit(solution)/shard_map/pallas_call | solution.py:218
  148.1 1.6 convolution_convert_fusion
  149.6 1.5 copy.50
  151.2 1.1 copy-done.9
  152.3 15.9 %shard_map.150 = (bf16[4,96,576]{2,1,0:T(8,128)(2,1)S(1)}, f32[8,8,128]{2,1,0:T(8,128)S(1)}, bf16[4,128,768]{2,1,0:T(8,128)(2,1)S(1)}, bf16[4,96,192]{2,1,0:T(8,128)(2,1)S(1)}) custom-call(bf16[4,2,96,576]{3,2,1,0:T(8,128)(2,1)S(1)} %bitcast.116, f32[8,8,128]{2,1,0:T(8,128)S(1)} %pad.9.refs_1_, bf16[4,128,768]{2,1,0:T(8,128)(2,1)S(1)} %bitcast.127, ...), custom_call_target="tpu_custom_call" | custom-call | tf_op jit(solution)/shard_map/pallas_call | solution.py:218
  168.3 12.5 %shard_map.151 = (f32[4,8,128]{2,1,0:T(8,128)S(1)}, bf16[4,96,576]{2,1,0:T(8,128)(2,1)S(1)}) custom-call(f32[8,128]{1,0:T(8,128)S(1)} %reduce_sum.234.refs_0_, bf16[4,96,576]{2,1,0:T(8,128)(2,1)S(1)} %fusion.4.refs_1_), custom_call_target="tpu_custom_call" | custom-call | tf_op jit(solution)/shard_map/pallas_call | solution.py:218
  183.3 1.7 add_convert_fusion
  (178 shorter events, 29.8 us)
Async XLA Ops:
  34.8 1.7 copy-start.19
  35.4 1.7 copy-start.27
  36.4 1.3 copy-start.42
  37.1 1.4 copy-start.22
  37.7 22.5 %copy-start.3 = (bf16[128,768]{1,0:T(8,128)(2,1)S(1)}, bf16[128,768]{1,0:T(8,128)(2,1)}, u32[]{:S(2)}) copy-start(bf16[128,768]{1,0:T(8,128)(2,1)} %refs_2_.1) | copy-start | bytes 589828
  60.1 4.0 %copy-start.12 = (bf16[8,96,288]{2,1,0:T(8,128)(2,1)}, bf16[8,96,288]{2,1,0:T(8,128)(2,1)S(1)}, u32[]{:S(2)}) copy-start(bf16[8,96,288]{2,1,0:T(8,128)(2,1)S(1)} %get-tuple-element.41) | copy-start | bytes 1327108
  60.1 4.0 %copy-start.18 = (bf16[96,288]{1,0:T(8,128)(2,1)S(1)}, bf16[96,288]{1,0:T(8,128)(2,1)}, u32[]{:S(2)}) copy-start(bf16[96,288]{1,0:T(8,128)(2,1)} %get-tuple-element.115.refs_1_) | copy-start | bytes 165892
  60.1 19.7 %copy-start.11 = (bf16[4,128,768]{2,1,0:T(8,128)(2,1)S(1)}, bf16[4,128,768]{2,1,0:T(8,128)(2,1)}, u32[]{:S(2)}) copy-start(bf16[4,128,768]{2,1,0:T(8,128)(2,1)} %copy-done.10) | copy-start | bytes 2359300
  60.3 1.3 copy-start.46
  61.7 18.0 %copy-start.45 = (f32[128]{0:T(128)}, f32[128]{0:T(128)S(1)}, u32[]{:S(2)}) copy-start(f32[128]{0:T(128)S(1)} %broadcast_multiply_fusion.11) | copy-start | bytes 1540
  62.9 16.9 %copy-start.48 = (f32[128]{0:T(128)}, f32[128]{0:T(128)S(1)}, u32[]{:S(2)}) copy-start(f32[128]{0:T(128)S(1)} %add_rsqrt_fusion.1) | copy-start | bytes 1540
  86.2 12.2 %copy-start.8 = (bf16[512,768]{1,0:T(8,128)(2,1)}, bf16[512,768]{1,0:T(8,128)(2,1)S(1)}, u32[]{:S(2)}) copy-start(bf16[512,768]{1,0:T(8,128)(2,1)S(1)} %get-tuple-element.50) | copy-start | bytes 2359300
  86.2 1.6 copy-start
  99.3 3.3 %copy-start.6 = (bf16[128,768]{1,0:T(8,128)(2,1)S(1)}, bf16[128,768]{1,0:T(8,128)(2,1)}, u32[]{:S(2)}) copy-start(bf16[128,768]{1,0:T(8,128)(2,1)} %refs_3_.1) | copy-start | bytes 589828
  99.3 5.2 %copy-start.1 = (bf16[768,896]{1,0:T(8,128)(2,1)S(1)}, bf16[768,896]{1,0:T(8,128)(2,1)}, u32[]{:S(2)}) copy-start(bf16[768,896]{1,0:T(8,128)(2,1)} %get-tuple-element.44) | copy-start | bytes 4128772
  102.6 18.0 %copy-start.23 = (bf16[3,64,512]{2,1,0:T(8,128)(2,1)S(1)}, bf16[3,64,512]{2,1,0:T(8,128)(2,1)}, u32[]{:S(2)}) copy-start(bf16[3,64,512]{2,1,0:T(8,128)(2,1)} %copy-done.22) | copy-start | bytes 589828
  125.7 2.1 %copy-start.20 = (f32[3,512,512]{1,2,0:T(8,128)S(1)}, f32[3,512,512]{1,2,0:T(8,128)}, u32[]{:S(2)}) copy-start(f32[3,512,512]{1,2,0:T(8,128)} %copy-done.19) | copy-start | bytes 9437188
  126.7 1.3 copy-start.28
  133.0 11.4 %copy-start.17 = (bf16[4,96,384]{2,1,0:T(8,128)(2,1)S(1)}, bf16[4,96,384]{2,1,0:T(8,128)(2,1)}, u32[]{:S(2)}) copy-start(bf16[4,96,384]{2,1,0:T(8,128)(2,1)} %copy-done.16) | copy-start | bytes 884740
  144.4 1.8 copy-start.21
  146.6 1.3 copy-start.26
  146.6 1.3 copy-start.37
  146.6 1.3 copy-start.39
  168.3 14.0 %copy-start.33 = (f32[128,768]{1,0:T(8,128)S(1)}, f32[128,768]{1,0:T(8,128)}, u32[]{:S(2)}) copy-start(f32[128,768]{1,0:T(8,128)} %get-tuple-element.93) | copy-start | bytes 1179652
  (26 other events, 24.1 us)

commit v4 on v3

--- a/solution.py
+++ b/solution.py
@@ -5,6 +5,7 @@
 from jax import lax
 from jax.experimental import pallas as pl
 from jax.experimental.pallas import tpu as pltpu
+from jax.experimental.layout import Layout, with_layout_constraint
 from jax.sharding import PartitionSpec as P
 
 HD = 64
@@ -240,6 +241,10 @@
     return jnp.sum(pieces.astype(jnp.float32), axis=0)
 
 
+def row_major(array):
+    return with_layout_constraint(array, Layout(major_to_minor=(0, 1)))
+
+
 def dot_f32(left, right, left_dim, right_dim):
     return lax.dot_general(
         left, right, (((left_dim,), (right_dim,)), ((), ())), preferred_element_type=jnp.float32
@@ -382,7 +387,7 @@
         ("outer", "dp", half_sum(mlp_grads, mlp_grads_a, 0, first)),
     )
     grad_hidden_rows = grad_hidden_rows.reshape(row_count, width)
-    grad_out_t = dot_f32(grad_hidden_rows, mixed_rows, 0, 0).astype(bf16)
+    grad_out_t = row_major(dot_f32(grad_hidden_rows, mixed_rows, 0, 0).astype(bf16))
     grad_mix = dot_f32(grad_hidden_rows, out_weight_t, 1, 0).astype(bf16).reshape(seq_shape)
     grad_q, grad_k, grad_v = over_sequences(
         attend_back, (queries, key_rows, value_rows, attn_mix, grad_mix, log_total)
@@ -395,34 +400,30 @@
         ],
         axis=1,
     ).astype(bf16)
-    grad_qkv = dot_f32(rows_one, grad_proj, 0, 0).astype(bf16)
+    grad_qkv = row_major(dot_f32(rows_one, grad_proj, 0, 0).astype(bf16))
     ln_one_part = dot_f32(grad_proj, qkv_weight, 1, 1).astype(bf16)
-    ln_one_parts, mlp_sums_b, grad_out_half = exchange(
+    ln_one_parts, mlp_sums_b, grad_out_half, qkv_half = exchange(
         sizes,
         5,
         ("scatter", "tensor", ln_one_part.reshape(members, own_rows, width)),
         ("outer", "dp", half_sum(mlp_grads, mlp_grads_b, first, mlp_wide)),
         ("half", "dp", quarter(grad_out_t)),
+        ("half", "dp", quarter(grad_qkv)),
     )
     grad_res_one, attn_gain_part = normalize_back(total_of(ln_one_parts), normed_one, inv_one, attn_full)
     input_grad = grad_hidden + grad_res_one
     gain_parts = jnp.stack([attn_gain_part, mlp_gain_part] + [jnp.zeros_like(attn_gain_part)] * 6)
     gain_parts = pad_columns(jnp.swapaxes(gain_parts.reshape(8, groups, block), 0, 1))
-    qkv_half, gain_parts, mlp_parts, grad_out_parts = exchange(
+    late_parts, gain_parts, mlp_parts, grad_out_parts = exchange(
         sizes,
         6,
-        ("half", "dp", quarter(grad_qkv)),
+        ("outer", "dp", half_sum(grad_qkv, qkv_half, 0, 3 * heads_wide)),
         ("scatter", "dp", gain_parts),
         ("scatter", "tensor", mlp_part.reshape(members, own_rows, width)),
         ("outer", "dp", half_sum(grad_out_t, grad_out_half, 0, heads_wide)),
     )
     output = (hidden_res + total_of(mlp_parts)).astype(bf16)
-    gain_groups, late_parts = exchange(
-        sizes,
-        7,
-        ("gather", "tensor", total_of(gain_parts)),
-        ("outer", "dp", half_sum(grad_qkv, qkv_half, 0, 3 * heads_wide)),
-    )
+    (gain_groups,) = exchange(sizes, 7, ("gather", "tensor", total_of(gain_parts)))
     gain_sum = total_of(gain_groups)
     late = total_of(late_parts)
     grad_w_qkv = jnp.stack([late[:, i * heads_wide : (i + 1) * heads_wide] for i in range(3)])

time: 187 us -> 178 us (0.952)
  local copies, waits for them, and re-layouts: 25 us -> 17.6 us
  Pallas kernels: 132 us -> 134 us
  other arithmetic: 18.3 us -> 16.4 us
    reshape x2 -> x0, local copies, waits for them, and re-layouts: 4.06 us -> none  [quarter(): return array.reshape(outer, 2, block, -1)]
    unnamed x105 -> x84, local copies, waits for them, and re-layouts: 16.2 us -> 14 us
    pallas_call x8, Pallas kernels: 127 us -> 129 us  [exchange(): pl.pallas_call(functools.partial(exchange_kernel, plan, sizes), out_shape...]
where the time goes in v4:
time: 178 us; the launch traced here: 177 us
  Pallas kernels  134 us (75%)
  local copies, waits for them, and re-layouts  17.6 us (10%)
  other arithmetic  16.4 us (9%)
  matrix products  7.65 us (4%)
    pallas_call x8, Pallas kernels, exchange(): pl.pallas_call(functools.partial(exchange_kernel, plan, sizes), out_shape...  129 us
    unnamed x84, local copies, waits for them, and re-layouts  14 us
    pallas_call x1, Pallas kernels, feed_forward(): pl.pallas_call(functools.partial(feed_forward_kernel, hidden), out_shape=...  5.41 us
    dot_general x6, matrix products, dot_f32(): lax.dot_general(left, right, (((left_dim,), (right_dim,)), ((), ())), pre...  3.84 us

profile of v4, /device:TPU:0, one launch (start us, length us, event | category | flops | bytes accessed | tf_op | source)
XLA Modules:
  0.0 176.9 jit_solution(3795170534750988899)
XLA Ops:
  0.6 0.9 copy.42
  3.2 0.9 copy-done.2
  4.1 0.9 copy-done.4
  5.0 24.9 %shard_map.143 = (bf16[8,96,768]{2,1,0:T(8,128)(2,1)S(1)}, bf16[8,16,128]{2,1,0:T(8,128)(2,1)S(1)}, bf16[4,128,768]{2,1,0:T(8,128)(2,1)S(1)}, bf16[4,128,768]{2,1,0:T(8,128)(2,1)S(1)}) custom-call(bf16[96,768]{1,0:T(8,128)(2,1)S(1)} %pad_maximum_fusion.6.refs_0_, bf16[16,128]{1,0:T(8,128)(2,1)S(1)} %fusion.40.refs_1_, bf16[128,768]{1,0:T(8,128)(2,1)S(1)} %copy-done.2, ...), custom_call_target="tpu_custom_call" | custom-call | tf_op jit(solution)/shard_map/pallas_call | solution.py:219
  32.6 1.0 broadcast_multiply_fusion.3
  35.1 1.1 copy-done.15
  40.7 21.4 %shard_map.144 = (bf16[4,128,768]{2,1,0:T(8,128)(2,1)S(1)}, bf16[8,96,288]{2,1,0:T(8,128)(2,1)S(1)}, bf16[8,96,288]{2,1,0:T(8,128)(2,1)S(1)}) custom-call(bf16[4,128,768]{2,1,0:T(8,128)(2,1)S(1)} %bitcast.117, bf16[96,288]{1,0:T(8,128)(2,1)S(1)} %copy-done.11, bf16[96,288]{1,0:T(8,128)(2,1)S(1)} %bitcast.136), custom_call_target="tpu_custom_call" | custom-call | tf_op jit(solution)/shard_map/pallas_call | solution.py:219
  63.1 1.3 fusion.51
  64.5 1.2 multiply_reduce_fusion.5
  65.7 1.1 multiply_convert_fusion.1.refs_0_
  66.8 15.6 %shard_map.145 = (bf16[4,128,768]{2,1,0:T(8,128)(2,1)S(1)}, bf16[8,96,288]{2,1,0:T(8,128)(2,1)S(1)}) custom-call(bf16[128,768]{1,0:T(8,128)(2,1)S(1)} %multiply_convert_fusion.1.refs_0_, bf16[96,288]{1,0:T(8,128)(2,1)S(1)} %copy-done.12), custom_call_target="tpu_custom_call" | custom-call | tf_op jit(solution)/shard_map/pallas_call | solution.py:219
  82.5 5.4 %shard_map.146 = (bf16[512,768]{1,0:T(8,128)(2,1)S(1)}, bf16[512,768]{1,0:T(8,128)(2,1)S(1)}, bf16[768,896]{1,0:T(8,128)(2,1)}) custom-call(bf16[512,768]{1,0:T(8,128)(2,1)S(1)} %bitcast.132, bf16[768,288]{1,0:T(8,128)(2,1)S(1)} %bitcast.133, bf16[768,288]{1,0:T(8,128)(2,1)S(1)} %bitcast.135, bf16[768,288]{1,0:T(8,128)(2,1)S(1)} %bitcast.134, ...), custom_call_target="tpu_custom_call" | custom-call | tf_op jit(solution)/shard_map/pallas_call | solution.py:281
  87.9 0.9 copy-done.6
  88.8 1.3 copy-done
  90.2 10.5 %shard_map.147 = (bf16[4,128,768]{2,1,0:T(8,128)(2,1)S(1)}, bf16[4,96,384]{2,1,0:T(8,128)(2,1)S(1)}) custom-call(bf16[4,128,768]{2,1,0:T(8,128)(2,1)S(1)} %bitcast.129, bf16[4,2,96,896]{3,2,1,0:T(8,128)(2,1)S(1)} %bitcast.113), custom_call_target="tpu_custom_call" | custom-call | tf_op jit(solution)/shard_map/pallas_call | solution.py:219
  101.6 0.9 fusion.50
  102.5 0.9 slice.130
  103.4 1.0 fusion.9.refs_2_
  104.5 14.6 %shard_map.148 = (bf16[4,128,768]{2,1,0:T(8,128)(2,1)S(1)}, bf16[4,96,512]{2,1,0:T(8,128)(2,1)S(1)}, bf16[4,96,384]{2,1,0:T(8,128)(2,1)S(1)}) custom-call(bf16[128,768]{1,0:T(8,128)(2,1)S(1)} %get-tuple-element.90.refs_0_, bf16[4,2,96,896]{3,2,1,0:T(8,128)(2,1)S(1)} %bitcast.115, bf16[4,96,384]{2,1,0:T(8,128)(2,1)S(1)} %fusion.9.refs_2_), custom_call_target="tpu_custom_call" | custom-call | tf_op jit(solution)/shard_map/pallas_call | solution.py:219
  127.0 18.5 %shard_map.149 = (bf16[4,128,768]{2,1,0:T(8,128)(2,1)S(1)}, bf16[4,96,512]{2,1,0:T(8,128)(2,1)S(1)}, bf16[4,96,192]{2,1,0:T(8,128)(2,1)S(1)}, bf16[4,96,576]{2,1,0:T(8,128)(2,1)S(1)}) custom-call(bf16[4,128,768]{2,1,0:T(8,128)(2,1)S(1)} %bitcast.131, bf16[4,96,512]{2,1,0:T(8,128)(2,1)S(1)} %fusion.8.refs_1_, bf16[4,2,96,192]{3,2,1,0:T(8,128)(2,1)S(1)} %bitcast.124, ...), custom_call_target="tpu_custom_call" | custom-call | tf_op jit(solution)/shard_map/pallas_call | solution.py:219
  146.5 0.9 add_rsqrt_fusion
  148.1 19.3 %shard_map.150 = (bf16[4,96,576]{2,1,0:T(8,128)(2,1)S(1)}, f32[8,8,128]{2,1,0:T(8,128)S(1)}, bf16[4,128,768]{2,1,0:T(8,128)(2,1)S(1)}, bf16[4,96,192]{2,1,0:T(8,128)(2,1)S(1)}) custom-call(bf16[4,96,576]{2,1,0:T(8,128)(2,1)S(1)} %fusion.4.refs_0_, f32[8,8,128]{2,1,0:T(8,128)S(1)} %pad.9.refs_1_, bf16[4,128,768]{2,1,0:T(8,128)(2,1)S(1)} %bitcast.128, ...), custom_call_target="tpu_custom_call" | custom-call | tf_op jit(solution)/shard_map/pallas_call | solution.py:219
  168.3 0.9 fusion.19
  169.3 3.7 %shard_map.151 = f32[4,8,128]{2,1,0:T(8,128)S(1)} custom-call(f32[8,128]{1,0:T(8,128)S(1)} %reduce_sum.234.refs_0_), custom_call_target="tpu_custom_call" | custom-call | tf_op jit(solution)/shard_map/pallas_call | solution.py:219
  (153 shorter events, 26.3 us)
Async XLA Ops:
  32.4 2.7 %copy-start.25 = (bf16[512,192]{0,1:T(8,128)(2,1)}, bf16[512,192]{0,1:T(8,128)(2,1)S(1)}, u32[]{:S(2)}) copy-start(bf16[512,192]{0,1:T(8,128)(2,1)S(1)} %slice.168) | copy-start | bytes 589828
  34.6 1.7 copy-start.15
  36.2 1.3 copy-start.34
  36.9 2.0 %copy-start.23 = (bf16[3,64,512]{2,1,0:T(8,128)(2,1)}, bf16[3,64,512]{2,1,0:T(8,128)(2,1)S(1)}, u32[]{:S(2)}) copy-start(bf16[3,64,512]{2,1,0:T(8,128)(2,1)S(1)} %convolution_convert_fusion.6) | copy-start | bytes 589828
  36.9 1.3 copy-start.35
  37.5 25.5 %copy-start.3 = (bf16[128,768]{1,0:T(8,128)(2,1)S(1)}, bf16[128,768]{1,0:T(8,128)(2,1)}, u32[]{:S(2)}) copy-start(bf16[128,768]{1,0:T(8,128)(2,1)} %refs_2_.1) | copy-start | bytes 589828
  62.1 2.3 %copy-start.37 = (f32[8,96]{1,0:T(8,128)S(1)}, f32[8,96]{1,0:T(8,128)}, u32[]{:S(2)}) copy-start(f32[8,96]{1,0:T(8,128)} %get-tuple-element.88) | copy-start | bytes 9220
  62.1 4.7 %copy-start.12 = (bf16[96,288]{1,0:T(8,128)(2,1)S(1)}, bf16[96,288]{1,0:T(8,128)(2,1)}, u32[]{:S(2)}) copy-start(bf16[96,288]{1,0:T(8,128)(2,1)} %get-tuple-element.113.refs_1_) | copy-start | bytes 165892
  63.0 19.4 %copy-start.9 = (bf16[8,96,288]{2,1,0:T(8,128)(2,1)S(1)}, bf16[8,96,288]{2,1,0:T(8,128)(2,1)}, u32[]{:S(2)}) copy-start(bf16[8,96,288]{2,1,0:T(8,128)(2,1)} %copy-done.8) | copy-start | bytes 1327108
  63.1 24.8 %copy-start.38 = (f32[128]{0:T(128)}, f32[128]{0:T(128)S(1)}, u32[]{:S(2)}) copy-start(f32[128]{0:T(128)S(1)} %broadcast_multiply_fusion.8) | copy-start | bytes 1540
  88.8 1.3 copy-start
  90.2 10.6 %copy-start.17 = (f32[128,768]{1,0:T(8,128)S(1)}, f32[128,768]{1,0:T(8,128)}, u32[]{:S(2)}) copy-start(f32[128,768]{1,0:T(8,128)} %get-tuple-element.93) | copy-start | bytes 1179652
  90.2 11.4 %copy-start.5 = (bf16[128,768]{1,0:T(8,128)(2,1)S(1)}, bf16[128,768]{1,0:T(8,128)(2,1)}, u32[]{:S(2)}) copy-start(bf16[128,768]{1,0:T(8,128)(2,1)} %refs_3_.1) | copy-start | bytes 589828
  101.6 2.9 %copy-start.1 = (bf16[768,896]{1,0:T(8,128)(2,1)S(1)}, bf16[768,896]{1,0:T(8,128)(2,1)}, u32[]{:S(2)}) copy-start(bf16[768,896]{1,0:T(8,128)(2,1)} %get-tuple-element.43) | copy-start | bytes 4128772
  104.5 15.2 %copy-start.16 = (f32[3,512,512]{1,2,0:T(8,128)S(1)}, f32[3,512,512]{1,2,0:T(8,128)}, u32[]{:S(2)}) copy-start(f32[3,512,512]{1,2,0:T(8,128)} %copy-done.15) | copy-start | bytes 9437188
  119.7 1.0 copy-start.26
  125.0 1.1 copy-start.22
  127.0 19.3 %copy-start.36 = (f32[768]{0:T(1024)S(1)}, f32[768]{0:T(1024)}, u32[]{:S(2)}) copy-start(f32[768]{0:T(1024)} %get-tuple-element.82) | copy-start | bytes 9220
  146.2 1.3 copy-start.39
  146.3 1.7 copy-start.14
  146.3 1.8 %copy-start.7 = (bf16[512,768]{1,0:T(8,128)(2,1)S(1)}, bf16[512,768]{1,0:T(8,128)(2,1)}, u32[]{:S(2)}) copy-start(bf16[512,768]{1,0:T(8,128)(2,1)} %copy-done.6) | copy-start | bytes 2359300
  148.0 19.6 %copy-start.18 = (f32[128,768]{1,0:T(8,128)S(1)}, f32[128,768]{1,0:T(8,128)}, u32[]{:S(2)}) copy-start(f32[128,768]{1,0:T(8,128)} %get-tuple-element.93) | copy-start | bytes 1179652
  148.1 20.2 %copy-start.20 = (f32[128,768]{1,0:T(8,128)S(1)}, f32[128,768]{1,0:T(8,128)}, u32[]{:S(2)}) copy-start(f32[128,768]{1,0:T(8,128)} %copy-done.19) | copy-start | bytes 1179652
  148.1 20.2 %copy-start.31 = (f32[128,768]{1,0:T(8,128)S(1)}, f32[128,768]{1,0:T(8,128)}, u32[]{:S(2)}) copy-start(f32[128,768]{1,0:T(8,128)} %get-tuple-element.91) | copy-start | bytes 1179652
  (16 other events, 14.0 us)
